TPU v7x, 128 devices: a whole 4x4x4 slice. The times are simulated.
128 devices in a mesh: dp: 8 (over x, core), seq: 16 (over z, y).
Axes of the slice: x: 4, y: 4, z: 4, core: 2. Of those that a mesh axis runs over, the one named last changes fastest.
Arguments:
- qkv: bfloat16 [3, 8, 2048, 16, 128], P(None, 'dp', 'seq'), may hold values from -6 to 6
- tile_mask: int32 [8, 16, 16], replicated, may hold values from 0 to 1, as said below
- d_out: bfloat16 [8, 2048, 3072], P('dp', 'seq'), may hold values from -6 to 6
- w_out: bfloat16 [16, 128, 3072], P('seq'), may hold values from -0.109375 to 0.109375
- momentum: float32 [16, 128, 3072], P('seq'), may hold values from -170 to 170
Outputs:
- grad_qkv: bfloat16 [3, 8, 2048, 16, 128], P(None, 'dp', 'seq')
- synced_momentum: bfloat16 [16, 128, 3072], P('seq')
- worker_error: float32 [8, 16, 128, 3072], P('dp', 'seq')
- server_error: float32 [16, 128, 3072], P('seq', 'dp')
Inputs may be any that keep to these rules, and one draw needn't show every extreme that they name: tile_mask[g, i, j] is 1 exactly when tiles i and j, numbered frame by frame over 4 frames of 2 by 2 tiles, differ by at most a per-group reach in frames (0 to 2), in tile rows (0 or 1) and in tile columns (0 or 1); every tile sees itself.
All inputs are finite; a program needn't handle non-finite values. Where the computation divides by a largest or mean magnitude, that divisor is 1e-20 or more.
Results may differ from a plain program's by a relative error of at most 0.0085.
Values may be sent and summed in bfloat16 or wider, within the bound.
A program may use at most 128 MiB of HBM per device.

v0:
```python
import math

import jax
import jax.numpy as jnp
from jax import lax
from jax.sharding import PartitionSpec as P

HEADS = 16
GROUPS = 8
TILE = 128


def body(qkv, tile_mask, d_out, w_out, momentum):
    seq_count = lax.axis_size("seq")
    worker_count = lax.axis_size("dp")
    tokens_here = qkv.shape[2]
    head_size = qkv.shape[4]
    length = tokens_here * seq_count
    heads_here = HEADS // seq_count
    inv_root = 1.0 / math.sqrt(head_size)
    block_rows = min(512, length)
    block_count = length // block_rows
    block_tiles = block_rows // TILE
    local = lax.all_to_all(qkv, "seq", split_axis=3, concat_axis=2, tiled=True)
    queries = local[0, 0]
    keys = local[1, 0]
    values = local[2, 0]
    head_ids = lax.axis_index("seq") * heads_here + jnp.arange(heads_here)
    group_ids = head_ids // (HEADS // GROUPS)
    picks = (group_ids[:, None] == jnp.arange(GROUPS)[None, :]).astype(jnp.int32)
    head_tiles = jnp.sum(picks[:, :, None, None] * tile_mask[None], axis=1)

    def block_probs(query_block, block_index):
        scores = (
            jnp.einsum("qhe,khe->hqk", query_block, keys, preferred_element_type=jnp.float32)
            * inv_root
        )
        row_tiles = lax.dynamic_slice_in_dim(head_tiles, block_index * block_tiles, block_tiles, 1)
        visible = jnp.repeat(jnp.repeat(row_tiles, TILE, axis=1), TILE, axis=2) > 0
        scores = jnp.where(visible, scores, -jnp.inf)
        row_top = jnp.max(scores, axis=-1, keepdims=True)
        expo = jnp.exp(scores - row_top)
        return expo / jnp.sum(expo, axis=-1, keepdims=True)

    def attend(probs):
        return jnp.einsum(
            "hqk,khe->qhe", probs.astype(jnp.bfloat16), values, preferred_element_type=jnp.float32
        ).astype(jnp.bfloat16)

    query_blocks = queries.reshape(block_count, block_rows, heads_here, head_size)
    block_ids = jnp.arange(block_count, dtype=jnp.int32)

    def forward_plain(inputs):
        return attend(block_probs(inputs[0], inputs[1]))

    attended_blocks = lax.map(forward_plain, (query_blocks, block_ids))
    attended = attended_blocks.reshape(length, heads_here, head_size)
    cot_local = d_out[0]
    token_out = lax.all_to_all(attended, "seq", split_axis=0, concat_axis=1, tiled=True)
    token_cot = jnp.einsum(
        "ld,hed->lhe",
        cot_local,
        lax.all_gather(w_out, "seq", axis=0, tiled=True),
        preferred_element_type=jnp.float32,
    ).astype(jnp.bfloat16)
    head_cot = lax.all_to_all(token_cot, "seq", split_axis=1, concat_axis=0, tiled=True)
    weight_grad = lax.psum_scatter(
        jnp.einsum("lhe,ld->hed", token_out, cot_local, preferred_element_type=jnp.float32).astype(
            jnp.bfloat16
        ),
        "seq",
        scatter_dimension=0,
        tiled=True,
    ).astype(jnp.float32)
    cot_blocks = head_cot.reshape(block_count, block_rows, heads_here, head_size)
    out_blocks = attended.reshape(block_count, block_rows, heads_here, head_size)

    def backward_plain(running, inputs):
        query_block, cot_block, out_block, block_index = inputs
        key_grad, value_grad = running
        probs = block_probs(query_block, block_index)
        probs_b = probs.astype(jnp.bfloat16)
        delta = jnp.sum(cot_block.astype(jnp.float32) * out_block.astype(jnp.float32), axis=-1)
        dprobs = jnp.einsum("qhe,khe->hqk", cot_block, values, preferred_element_type=jnp.float32)
        dscores = (probs * (dprobs - jnp.transpose(delta)[:, :, None])).astype(jnp.bfloat16)
        query_grad = (
            jnp.einsum("hqk,khe->qhe", dscores, keys, preferred_element_type=jnp.float32) * inv_root
        ).astype(jnp.bfloat16)
        key_grad = key_grad + jnp.einsum(
            "hqk,qhe->khe", dscores, query_block, preferred_element_type=jnp.float32
        )
        value_grad = value_grad + jnp.einsum(
            "hqk,qhe->khe", probs_b, cot_block, preferred_element_type=jnp.float32
        )
        return ((key_grad, value_grad), query_grad)

    start_pair = (
        jnp.zeros((length, heads_here, head_size), jnp.float32),
        jnp.zeros((length, heads_here, head_size), jnp.float32),
    )
    (key_grad, value_grad), query_grads = lax.scan(
        backward_plain, start_pair, (query_blocks, cot_blocks, out_blocks, block_ids)
    )
    head_grads = jnp.stack(
        [
            query_grads.reshape(length, heads_here, head_size),
            (key_grad * inv_root).astype(jnp.bfloat16),
            value_grad.astype(jnp.bfloat16),
        ]
    )[:, None]
    grad_qkv = lax.all_to_all(head_grads, "seq", split_axis=2, concat_axis=3, tiled=True)
    worker_mom = 0.9 * momentum + 0.1 * weight_grad
    worker_scale = jnp.mean(jnp.abs(worker_mom), axis=(1, 2), keepdims=True) + 1e-06
    sent = (worker_scale * jnp.tanh(worker_mom / worker_scale)).astype(jnp.bfloat16)
    worker_error = (worker_mom - sent.astype(jnp.float32))[None]
    received = lax.all_to_all(sent[None], "dp", split_axis=2, concat_axis=0, tiled=True)
    averaged = jnp.sum(received.astype(jnp.float32), axis=0) / worker_count
    server_scale = jnp.mean(jnp.abs(averaged), axis=(1, 2), keepdims=True) + 1e-06
    server_sent = (server_scale * jnp.tanh(averaged / server_scale)).astype(jnp.bfloat16)
    server_error = averaged - server_sent.astype(jnp.float32)
    synced_momentum = lax.all_gather(server_sent, "dp", axis=1, tiled=True)
    return (grad_qkv, synced_momentum, worker_error, server_error)


def solution(mesh):
    placed = (
        P(None, "dp", "seq", None, None),
        P(),
        P("dp", "seq", None),
        P("seq", None, None),
        P("seq", None, None),
    )
    return jax.shard_map(
        body,
        mesh=mesh,
        in_specs=placed,
        out_specs=(
            P(None, "dp", "seq", None, None),
            P("seq", None, None),
            P("dp", "seq", None, None),
            P("seq", "dp", None),
        ),
        check_vma=False,
    )
```

profile of v0, /device:TPU:49, one launch (start us, length us, event | category | flops | bytes accessed | tf_op | source)
XLA Modules:
  0.0 304.3 jit_solution(2157953456725174847)
XLA Ops:
  7.9 3.0 copy.34
  10.9 7.4 %all-to-all-start = ((bf16[3,1,128,16,128]{4,2,0,1,3:T(8,128)(2,1)}), bf16[3,1,128,16,128]{4,2,0,1,3:T(8,128)(2,1)S(1)}, u32[]{:S(2)}, u32[]{:S(2)}) async-start(bf16[3,1,128,16,128]{4,2,0,1,3:T(8,128)(2,1)} %copy.34), calls=%async_computation | async-start | bytes 3145728 | tf_op jit(solution)/shard_map/all_to_all | solution.py:24
  18.4 27.2 %all-to-all-done = bf16[3,1,128,16,128]{4,2,0,1,3:T(8,128)(2,1)S(1)} async-done(((bf16[3,1,128,16,128]{4,2,0,1,3:T(8,128)(2,1)}), bf16[3,1,128,16,128]{4,2,0,1,3:T(8,128)(2,1)S(1)}, u32[]{:S(2)}, u32[]{:S(2)}) %all-to-all-start) | async-done | bytes 1572896 | tf_op jit(solution)/shard_map/all_to_all | solution.py:24
  46.1 30.0 %while.25 = (s32[]{:T(128)}, bf16[4,512,1,128]{3,1,2,0:T(8,128)(2,1)S(1)}, s32[4]{0:T(128)S(1)}, s32[1,16,16]{2,1,0:T(8,128)S(1)}, bf16[4,512,1,128]{3,1,2,0:T(8...) while((s32[]{:T(128)}, ...), condition=%wide.region_4.5_spmd, body=%wide.region_1.4_spmd.sunk | while | flops 545324096 | bytes 16017979 | solution.py:56
  47.4 3.5 %broadcast_in_dim.59 = pred[512,16,128]{2,1,0:T(8,128)(4,1)S(1)} broadcast(pred[512,16]{1,0:T(8,128)(4,1)S(1)} %bitcast.202), dimensions={0,1} | broadcast | bytes 1056768 | tf_op jit(solution)/shard_map/while/body/eval_jaxpr/broadcast_in_dim | solution.py:39
  50.8 1.1 fusion.71
  51.9 0.7 fusion.72
  52.6 0.9 fusion.73
  54.9 3.5 %broadcast_in_dim.59 = pred[512,16,128]{2,1,0:T(8,128)(4,1)S(1)} broadcast(pred[512,16]{1,0:T(8,128)(4,1)S(1)} %bitcast.202), dimensions={0,1} | broadcast | bytes 1056768 | tf_op jit(solution)/shard_map/while/body/eval_jaxpr/broadcast_in_dim | solution.py:39
  58.3 1.1 fusion.71
  60.1 0.9 fusion.73
  62.4 3.5 %broadcast_in_dim.59 = pred[512,16,128]{2,1,0:T(8,128)(4,1)S(1)} broadcast(pred[512,16]{1,0:T(8,128)(4,1)S(1)} %bitcast.202), dimensions={0,1} | broadcast | bytes 1056768 | tf_op jit(solution)/shard_map/while/body/eval_jaxpr/broadcast_in_dim | solution.py:39
  65.8 1.1 fusion.71
  67.6 0.9 fusion.73
  69.9 3.5 %broadcast_in_dim.59 = pred[512,16,128]{2,1,0:T(8,128)(4,1)S(1)} broadcast(pred[512,16]{1,0:T(8,128)(4,1)S(1)} %bitcast.202), dimensions={0,1} | broadcast | bytes 1056768 | tf_op jit(solution)/shard_map/while/body/eval_jaxpr/broadcast_in_dim | solution.py:39
  73.4 1.1 fusion.71
  74.4 0.7 fusion.72
  75.1 0.9 fusion.73
  76.1 0.8 copy-done.7
  77.5 1.0 reduce.17
  78.6 19.5 %all_to_all.75 = bf16[16,2,8192]{2,1,0:T(2,128)(2,1)S(1)} all-to-all(bf16[16,2,8192]{2,1,0:T(2,128)(2,1)S(1)} %reshape.279), channel_id=1, replica_groups=mesh['dp'=8,'seq'=16] {'seq'}, dimensions={0} | all-to-all | bytes 1048576 | tf_op jit(solution)/shard_map/all_to_all | solution.py:59
  99.0 6.4 %convolution_convert_fusion = bf16[16,128,3072]{2,1,0:T(8,128)(2,1)} fusion(bf16[1,128,3072]{2,1,0:T(8,128)(2,1)S(1)} %copy-done, bf16[16,128,1,128]{1,3,0,2:T(8,128)(2,1)S(1)} %copy.44), kind=kOutput, calls=%fused_computation.47 | convolution fusion | flops 1616904192 | bytes 13893632 | tf_op jit(solution)/shard_map/lhe,ld->hed/dot_general | solution.py:68
  105.4 12.6 %all-gather.2.cloned.1.call-done = bf16[16,128,3072]{2,1,0:T(8,128)(2,1)} async-done(((bf16[1,128,3072]{2,1,0:T(8,128)(2,1)}), bf16[16,128,3072]{2,1,0:T(8,128)(2,1)}) %all-gather.2.cloned.1.call-update) | async-done | bytes 12582928 | tf_op jit(solution)/shard_map/all_gather | solution.py:63
  118.0 8.0 %convolution_convert_fusion.1 = bf16[128,16,128]{2,0,1:T(8,128)(2,1)} fusion(bf16[16,128,3072]{2,1,0:T(8,128)(2,1)} %all-gather.2.cloned.1.call-done, bf16[1,128,3072]{2,1,0:T(8,128)(2,1)S(1)} %copy-done), kind=kOutput, calls=%fused_computation.54 | convolution fusion | flops 1610874880 | bytes 13893632 | tf_op jit(solution)/shard_map/ld,hed->lhe/dot_general | solution.py:60
  126.0 6.5 %all-to-all-start.1 = ((bf16[128,16,128]{2,0,1:T(8,128)(2,1)}), bf16[128,16,128]{2,0,1:T(8,128)(2,1)S(1)}, u32[]{:S(2)}, u32[]{:S(2)}) async-start(bf16[128,16,128]{2,0,1:T(8,128)(2,1)} %convolution_convert_fusion.1), calls=%async_computation.1 | async-start | bytes 1048576 | tf_op jit(solution)/shard_map/all_to_all | solution.py:66
  132.4 12.3 %all-to-all-done.1 = bf16[128,16,128]{2,0,1:T(8,128)(2,1)S(1)} async-done(((bf16[128,16,128]{2,0,1:T(8,128)(2,1)}), bf16[128,16,128]{2,0,1:T(8,128)(2,1)S(1)}, u32[]{:S(2)}, u32[]{:S(2)}) %all-to-all-start.1) | async-done | bytes 524320 | tf_op jit(solution)/shard_map/all_to_all | solution.py:66
  144.8 49.1 %while.26 = (s32[]{:T(128)}, f32[2048,1,128]{0,2,1:T(8,128)S(1)}, f32[2048,1,128]{0,2,1:T(8,128)}, bf16[4,512,1,128]{3,1,2,0:T(8,128)(2,1)S(1)}, bf16[4,512,1,12...) while((s32[]{:T(128)}, f32[2048,1,128]{0,2,1:T(8,128)S(1)}, ...), condition=%wide.region_9.10_spmd.clone, body=%wide.region_5.9_spmd.clone.sunk | while | flops 1357249024 | bytes 44468964 | solution.py:101
  146.2 3.5 %broadcast_in_dim.61 = pred[512,16,128]{2,1,0:T(8,128)(4,1)S(1)} broadcast(pred[512,16]{1,0:T(8,128)(4,1)S(1)} %bitcast.203), dimensions={0,1} | broadcast | bytes 1056768 | tf_op jit(solution)/shard_map/while/body/eval_jaxpr/broadcast_in_dim | solution.py:39
  149.7 2.2 fusion.83
  153.2 1.1 fusion.86
  154.3 1.2 multiply_convert_fusion.4
  155.7 0.8 fusion.87
  158.5 3.5 %broadcast_in_dim.61 = pred[512,16,128]{2,1,0:T(8,128)(4,1)S(1)} broadcast(pred[512,16]{1,0:T(8,128)(4,1)S(1)} %bitcast.203), dimensions={0,1} | broadcast | bytes 1056768 | tf_op jit(solution)/shard_map/while/body/eval_jaxpr/broadcast_in_dim | solution.py:39
  162.0 2.2 fusion.83
  165.5 1.1 fusion.86
  166.7 1.2 multiply_convert_fusion.4
  168.1 0.8 fusion.87
  170.9 3.5 %broadcast_in_dim.61 = pred[512,16,128]{2,1,0:T(8,128)(4,1)S(1)} broadcast(pred[512,16]{1,0:T(8,128)(4,1)S(1)} %bitcast.203), dimensions={0,1} | broadcast | bytes 1056768 | tf_op jit(solution)/shard_map/while/body/eval_jaxpr/broadcast_in_dim | solution.py:39
  174.3 2.2 fusion.83
  177.8 1.1 fusion.86
  178.9 1.2 multiply_convert_fusion.4
  180.3 0.8 fusion.87
  183.1 3.5 %broadcast_in_dim.61 = pred[512,16,128]{2,1,0:T(8,128)(4,1)S(1)} broadcast(pred[512,16]{1,0:T(8,128)(4,1)S(1)} %bitcast.203), dimensions={0,1} | broadcast | bytes 1056768 | tf_op jit(solution)/shard_map/while/body/eval_jaxpr/broadcast_in_dim | solution.py:39
  186.6 2.1 fusion.83
  190.0 1.1 fusion.86
  191.1 1.2 multiply_convert_fusion.4
  192.5 0.8 fusion.87
  193.9 1.5 copy.40
  196.0 10.8 %copy.41 = bf16[3,1,2048,1,128]{4,0,3,1,2:T(4,128)(2,1)} copy(bf16[3,1,2048,1,128]{4,2,0,3,1:T(8,128)(2,1)S(1)} %maximum_bitcast_fusion) | data formatting | bytes 3145728 | tf_op jit(solution)/shard_map/broadcast_in_dim | solution.py:104
  206.8 7.9 %all-to-all-start.2 = ((bf16[3,1,2048,1,128]{4,0,3,1,2:T(4,128)(2,1)}), bf16[3,1,2048,1,128]{4,0,3,1,2:T(4,128)(2,1)S(1)}, u32[]{:S(2)}, u32[]{:S(2)}) async-start(bf16[3,1,2048,1,128]{4,0,3,1,2:T(4,128)(2,1)} %copy.41), calls=%async_computation.2 | async-start | bytes 4194304 | tf_op jit(solution)/shard_map/all_to_all | solution.py:111
  214.7 14.0 %reduce-scatter.4.cloned.1.call-done = bf16[1,128,3072]{2,1,0:T(8,128)(2,1)} async-done(((bf16[16,128,3072]{2,1,0:T(8,128)(2,1)}), bf16[1,128,3072]{2,1,0:T(8,128)(2,1)}) %reduce-scatter.4.cloned.1.call-update) | async-done | bytes 786448
  228.7 2.7 abs_reduce_fusion
  232.1 3.0 subtract_bitcast_fusion
  235.1 2.4 copy.56
  237.4 6.4 %reduce.18 = bf16[128,3072]{1,0:T(8,128)(2,1)S(1)} reduce(bf16[128,1,1,3072]{3,2,1,0:T(2,128)(2,1)} %bitcast.205, bf16[]{:T(256)} %broadcast.159), dimensions={1,2}, to_apply=%bitcast.151.reduce_sub_computation | reduce | bytes 1572866
  243.8 1.5 reshape.281
  245.3 18.0 %all-to-all-start.4 = ((bf16[8,2,24576]{2,1,0:T(2,128)(2,1)}), bf16[8,2,24576]{2,1,0:T(2,128)(2,1)S(1)}, u32[]{:S(2)}, u32[]{:S(2)}) async-start(bf16[8,2,24576]{2,1,0:T(2,128)(2,1)} %reshape.281), calls=%async_computation.4 | async-start | bytes 1572864 | tf_op jit(solution)/shard_map/all_to_all | solution.py:116
  263.5 2.2 copy.46
  265.6 9.8 %all-to-all-done.4 = bf16[8,2,24576]{2,1,0:T(2,128)(2,1)S(1)} async-done(((bf16[8,2,24576]{2,1,0:T(2,128)(2,1)}), bf16[8,2,24576]{2,1,0:T(2,128)(2,1)S(1)}, u32[]{:S(2)}, u32[]{:S(2)}) %all-to-all-start.4) | async-done | bytes 786464 | tf_op jit(solution)/shard_map/all_to_all | solution.py:116
  275.4 3.2 %reshape.282 = bf16[128,1,1,3072]{3,2,1,0:T(2,128)(2,1)} reshape(bf16[8,2,24576]{2,1,0:T(2,128)(2,1)S(1)} %all-to-all-done.4) | data formatting | bytes 1572864
  278.6 1.7 copy.48
  281.7 0.7 bitcast_subtract_fusion
  282.4 14.2 %all_gather.7 = bf16[1,128,3072]{2,1,0:T(8,128)(2,1)S(1)} all-gather(bf16[1,16,3072]{2,1,0:T(8,128)(2,1)S(1)} %get-tuple-element.263), channel_id=1, replica_groups=mesh['dp'=8,'seq'=16] {'dp'}, dimensions={1}, use_global_device_ids=true | all-gather | bytes 884736 | tf_op jit(solution)/shard_map/all_gather | solution.py:121
  296.6 0.9 copy.79
  (107 shorter events, 19.8 us)
Async XLA Ops:
  7.2 91.8 %copy-start = (bf16[1,128,3072]{2,1,0:T(8,128)(2,1)S(1)}, bf16[1,128,3072]{2,1,0:T(8,128)(2,1)}, u32[]{:S(2)}) copy-start(bf16[1,128,3072]{2,1,0:T(8,128)(2,1)} %param.11) | copy-start | bytes 2359300
  7.2 110.8 %all-gather.2.cloned.1.call-start = ((), (), s32[]{:S(2)}) async-start(), calls=%async_computation.6 | async-start | bytes 13369344 | tf_op jit(solution)/shard_map/all_gather | solution.py:63
  10.9 7.5 %copy-start.9 = (s32[8,16,16]{2,1,0:T(8,128)S(1)}, s32[8,16,16]{2,1,0:T(8,128)}, u32[]{:S(2)}) copy-start(s32[8,16,16]{2,1,0:T(8,128)} %param.10) | copy-start | bytes 24580
  10.9 34.7 %all-to-all-start = ((bf16[3,1,128,16,128]{4,2,0,1,3:T(8,128)(2,1)}), bf16[3,1,128,16,128]{4,2,0,1,3:T(8,128)(2,1)S(1)}, u32[]{:S(2)}, u32[]{:S(2)}) async-start(bf16[3,1,128,16,128]{4,2,0,1,3:T(8,128)(2,1)} %copy.34), calls=%async_computation | async-start | bytes 3145728 | tf_op jit(solution)/shard_map/all_to_all | solution.py:24
  18.3 210.4 %reduce-scatter.4.cloned.1.call-start = ((), (), s32[]{:S(2)}) async-start(), calls=%async_computation.7 | async-start | bytes 13369344
  76.1 0.8 copy-start.7
  76.1 1.4 copy-start.5
  126.0 18.7 %all-to-all-start.1 = ((bf16[128,16,128]{2,0,1:T(8,128)(2,1)}), bf16[128,16,128]{2,0,1:T(8,128)(2,1)S(1)}, u32[]{:S(2)}, u32[]{:S(2)}) async-start(bf16[128,16,128]{2,0,1:T(8,128)(2,1)} %convolution_convert_fusion.1), calls=%async_computation.1 | async-start | bytes 1048576 | tf_op jit(solution)/shard_map/all_to_all | solution.py:66
  151.9 1.3 copy-start.3
  153.2 1.1 copy-start.6
  154.3 1.2 copy-start.4
  154.3 1.4 copy-start.8
  164.2 1.3 copy-start.3
  165.5 1.1 copy-start.6
  166.6 1.2 copy-start.4
  166.6 1.4 copy-start.8
  176.5 1.3 copy-start.3
  177.8 1.1 copy-start.6
  178.9 1.2 copy-start.4
  178.9 1.4 copy-start.8
  188.7 1.3 copy-start.3
  190.0 1.1 copy-start.6
  191.1 1.2 copy-start.4
  191.1 1.4 copy-start.8
  206.8 38.5 %all-to-all-start.2 = ((bf16[3,1,2048,1,128]{4,0,3,1,2:T(4,128)(2,1)}), bf16[3,1,2048,1,128]{4,0,3,1,2:T(4,128)(2,1)S(1)}, u32[]{:S(2)}, u32[]{:S(2)}) async-start(bf16[3,1,2048,1,128]{4,0,3,1,2:T(4,128)(2,1)} %copy.41), calls=%async_computation.2 | async-start | bytes 4194304 | tf_op jit(solution)/shard_map/all_to_all | solution.py:111
  228.7 3.4 %copy-start.2 = (bf16[1,128,3072]{2,1,0:T(8,128)(2,1)S(1)}, bf16[1,128,3072]{2,1,0:T(8,128)(2,1)}, u32[]{:S(2)}) copy-start(bf16[1,128,3072]{2,1,0:T(8,128)(2,1)} %reduce-scatter.4.cloned.1.call-done) | copy-start | bytes 2359300
  245.3 30.2 %all-to-all-start.4 = ((bf16[8,2,24576]{2,1,0:T(2,128)(2,1)}), bf16[8,2,24576]{2,1,0:T(2,128)(2,1)S(1)}, u32[]{:S(2)}, u32[]{:S(2)}) async-start(bf16[8,2,24576]{2,1,0:T(2,128)(2,1)} %reshape.281), calls=%async_computation.4 | async-start | bytes 1572864 | tf_op jit(solution)/shard_map/all_to_all | solution.py:116
  280.3 17.2 %copy-start.1 = (bf16[1,128,3072]{2,1,0:T(8,128)(2,1)S(1)}, bf16[1,128,3072]{2,1,0:T(8,128)(2,1)}, u32[]{:S(2)}) copy-start(bf16[1,128,3072]{2,1,0:T(8,128)(2,1)} %param.11) | copy-start | bytes 2359300
Sparse Core Ops, SparseCore 0:
  10.1 107.8 all-gather.1
  121.4 107.2 reduce-scatter.3
where the time goes:
time: 306 us; the launch traced here: 304 us
  waiting for transfers between devices  76.5 us (25%)
  local copies, waits for them, and re-layouts  66.2 us (22%)
  matrix products  45.4 us (15%)
  starting transfers between devices  39.8 us (13%)
  blocking collectives  33.7 us (11%)
  other arithmetic  21.3 us (7%)
  between operations  15.6 us (5%)
  loops' own time  5.83 us (2%)
    broadcast_in_dim x16, local copies, waits for them, and re-layouts, block_probs(): visible = jnp.repeat(jnp.repeat(row_tiles, TILE, axis=1), TILE, axis=2) > 0  27.9 us
    all_to_all x1, waiting for transfers between devices, body(): local = lax.all_to_all(qkv, 'seq', split_axis=3, concat_axis=2, tiled=True)  27.2 us
    all_to_all x1, blocking collectives, body(): lax.all_to_all(attended, 'seq', split_axis=0, concat_axis=1, tiled=True)  19.5 us
    all_to_all x1, starting transfers between devices, body(): lax.all_to_all(sent[None], 'dp', split_axis=2, concat_axis=0, tiled=True)  18 us
    unnamed x3, waiting for transfers between devices  14.7 us
    all_gather x1, blocking collectives, body(): synced_momentum = lax.all_gather(server_sent, 'dp', axis=1, tiled=True)  14.2 us
    unnamed x21, local copies, waits for them, and re-layouts  13.8 us
    dot_general x8, matrix products, block_probs(): jnp.einsum('qhe,khe->hqk', query_block, keys, preferred_element_type=jnp....  13 us
  transfers between devices with their start and end apart: 6, of which 5 were waited for; matrix products, arithmetic and copies ran while one was open for 40% of the time, Pallas kernels for 0%

commit v1 on v0

v1 whole, which is shorter than its diff:
```python
import functools
import math

import jax
import jax.numpy as jnp
from jax import lax
from jax.experimental import pallas as pl
from jax.experimental.pallas import tpu as pltpu
from jax.sharding import PartitionSpec as P

HEADS = 16
GROUPS = 8
TILE = 128
SIDE = 4
BLOCKS = SIDE * SIDE
HALF = TILE // 2
MESH = pl.DeviceIdType.MESH

ORDER = (
    (0, 0),
    (-1, 0), (1, 0), (0, -1), (0, 1),
    (-1, -1), (-1, 1), (1, -1), (1, 1),
    (2, 0), (0, 2),
    (2, -1), (2, 1), (-1, 2), (1, 2),
    (2, 2),
)
COLUMNS = (0, -1, 1, 2)


def wrap(position, offset):
    return lax.rem(position + (offset + SIDE), SIDE)


def pick(step, table):
    value = jnp.int32(table[0])
    for index, entry in enumerate(table):
        if index and entry != table[0]:
            value = jnp.where(step == index, jnp.int32(entry), value)
    return value


def nt(a, b):
    return lax.dot_general(a, b, (((1,), (1,)), ((), ())), preferred_element_type=jnp.float32)


def nn(a, b):
    return lax.dot_general(a, b, (((1,), (0,)), ((), ())), preferred_element_type=jnp.float32)


def tn(a, b):
    return lax.dot_general(a, b, (((0,), (0,)), ((), ())), preferred_element_type=jnp.float32)


class Gather:
    def __init__(self, buf, z, y, z_first, row0, sem0, send, recv):
        self.buf, self.z, self.y, self.z_first = buf, z, y, z_first
        self.row0, self.sem0, self.send, self.recv = row0, sem0, send, recv

    def block(self, a, b):
        dz, dy = (a, b) if self.z_first else (b, a)
        return wrap(self.z, dz) * SIDE + wrap(self.y, dy)

    def peer(self, a, b):
        return {"seq": self.block(a, b)}

    def copy(self, slot, block, lo, n, a, b):
        rows = self.buf.at[block, pl.ds(self.row0 + lo, n)]
        return pltpu.make_async_remote_copy(
            src_ref=rows,
            dst_ref=rows,
            send_sem=self.send.at[self.sem0 + slot],
            recv_sem=self.recv.at[self.sem0 + slot],
            device_id=self.peer(a, b),
            device_id_type=MESH,
        )

    def first(self, kind):
        if kind == 0:
            return self.copy(0, self.block(0, 0), 0, HALF, 1, 0)
        if kind == 1:
            return self.copy(1, self.block(0, 0), 0, HALF, -1, 0)
        if kind == 2:
            return self.copy(2, self.block(-1, 0), 0, HALF // 2, 1, 0)
        return self.copy(3, self.block(1, 0), HALF // 2, HALF // 2, -1, 0)

    def second(self, column, kind):
        slot = 4 + 4 * COLUMNS.index(column) + kind
        if kind == 0:
            return self.copy(slot, self.block(column, 0), 0, HALF, 0, 1)
        if kind == 1:
            return self.copy(slot, self.block(column, 0), 0, HALF, 0, -1)
        if kind == 2:
            return self.copy(slot, self.block(column, -1), 0, HALF // 2, 0, 1)
        return self.copy(slot, self.block(column, 1), HALF // 2, HALF // 2, 0, -1)


def kernel(
    inv_root,
    qkv_ref, dout_ref, w_ref, mask_ref,
    grads_ref, gw_ref,
    qkvbuf, dbuf, bias, dkt, dvt,
    q_send, q_recv, d_send, d_recv, local_sem,
):
    me = lax.axis_index("seq")
    z = me // SIDE
    y = lax.rem(me, SIDE)
    peers = [
        wrap(z, dz) * SIDE + wrap(y, dy)
        for dz in range(SIDE) for dy in range(SIDE) if (dz, dy) != (0, 0)
    ]
    sources = [
        wrap(z, -dz) * SIDE + wrap(y, -dy)
        for dz in range(SIDE) for dy in range(SIDE) if (dz, dy) != (0, 0)
    ]

    own_d = pltpu.make_async_copy(dout_ref, dbuf.at[me], local_sem.at[0])
    own_d.start()
    own_q = pltpu.make_async_copy(
        qkv_ref.at[:, me], qkvbuf.at[:, pl.ds(me * TILE, TILE)], local_sem.at[1]
    )
    own_q.start()

    barrier = pltpu.get_barrier_semaphore()
    for peer in peers:
        pl.semaphore_signal(barrier, inc=1, device_id={"seq": peer}, device_id_type=MESH)
    pl.semaphore_wait(barrier, len(peers))

    q_copies = []
    for index, peer in enumerate(peers):
        copy = pltpu.make_async_remote_copy(
            src_ref=qkv_ref.at[:, peer],
            dst_ref=qkvbuf.at[:, pl.ds(me * TILE, TILE)],
            send_sem=q_send.at[index],
            recv_sem=q_recv.at[index],
            device_id={"seq": peer},
            device_id_type=MESH,
        )
        copy.start()
        q_copies.append(copy)

    halves = (
        Gather(dbuf, z, y, True, 0, 0, d_send, d_recv),
        Gather(dbuf, z, y, False, HALF, 20, d_send, d_recv),
    )
    own_d.wait()
    for g in halves:
        g.first(0).start()
        g.first(1).start()
    for g in halves:
        g.second(0, 0).start()
        g.second(0, 1).start()

    group = me // (HEADS // GROUPS)
    tiles = mask_ref[group]
    for j in range(BLOCKS):
        bias[:, j * TILE:(j + 1) * TILE] = jnp.broadcast_to(
            jnp.where(tiles[:, j:j + 1] > 0, 0.0, -jnp.inf), (BLOCKS, TILE)
        )
    dkt[...] = jnp.zeros_like(dkt)
    dvt[...] = jnp.zeros_like(dvt)
    gw_ref[...] = jnp.zeros_like(gw_ref)

    own_q.wait()
    for index, copy in enumerate(q_copies):
        copy.wait_recv()

    def arrive(step):
        if step == 1:
            for g in halves:
                g.first(0).wait_recv()
                g.first(2).start()
                g.second(-1, 0).start()
                g.second(-1, 1).start()
            for g in halves:
                g.first(1).wait_recv()
                g.first(3).start()
                g.second(1, 0).start()
                g.second(1, 1).start()
            for g in halves:
                g.second(0, 0).wait_recv()
                g.second(0, 2).start()
                g.second(0, 1).wait_recv()
                g.second(0, 3).start()
        elif step == 2:
            for g in halves:
                g.first(2).wait_recv()
                g.first(3).wait_recv()
                g.second(2, 0).start()
                g.second(2, 1).start()
        elif step == 5:
            for column in (-1, 1):
                for g in halves:
                    g.second(column, 0).wait_recv()
                    g.second(column, 2).start()
                    g.second(column, 1).wait_recv()
                    g.second(column, 3).start()
        elif step == 9:
            for g in halves:
                g.second(0, 2).wait_recv()
                g.second(0, 3).wait_recv()
        elif step == 11:
            for g in halves:
                g.second(2, 0).wait_recv()
                g.second(2, 2).start()
                g.second(2, 1).wait_recv()
                g.second(2, 3).start()
            for column in (-1, 1):
                for g in halves:
                    g.second(column, 2).wait_recv()
                    g.second(column, 3).wait_recv()
        elif step == 15:
            for g in halves:
                g.second(2, 2).wait_recv()
                g.second(2, 3).wait_recv()

    def body(step, carry):
        for number in (1, 2, 5, 9, 11, 15):
            @pl.when(step == number)
            def _():
                arrive(number)

        block = wrap(z, pick(step, [o[0] for o in ORDER])) * SIDE + wrap(
            y, pick(step, [o[1] for o in ORDER])
        )
        row0 = pl.multiple_of(block * TILE, TILE)
        q = qkvbuf[0, pl.ds(row0, TILE), :]
        k = qkvbuf[1]
        v = qkvbuf[2]
        d = dbuf[block]
        cot = nt(d, w_ref[...]).astype(jnp.bfloat16)
        scores = nt(q, k) * inv_root + bias[pl.ds(block, 1), :]
        top = jnp.max(scores, axis=-1, keepdims=True)
        expo = jnp.exp(scores - top)
        probs = expo * (1.0 / jnp.sum(expo, axis=-1, keepdims=True))
        probs_b = probs.astype(jnp.bfloat16)
        att = nn(probs_b, v).astype(jnp.bfloat16)
        delta = jnp.sum(
            cot.astype(jnp.float32) * att.astype(jnp.float32), axis=-1, keepdims=True
        )
        dscores = (probs * (nt(cot, v) - delta)).astype(jnp.bfloat16)
        grads_ref[0, pl.ds(row0, TILE), :] = (nn(dscores, k) * inv_root).astype(jnp.bfloat16)
        dkt[...] += tn(q, dscores)
        dvt[...] += tn(cot, probs_b)
        gw_ref[...] += tn(att, d)
        return carry

    lax.fori_loop(0, BLOCKS, body, 0)
    grads_ref[1] = (dkt[...].T * inv_root).astype(jnp.bfloat16)
    grads_ref[2] = dvt[...].T.astype(jnp.bfloat16)

    for copy in q_copies:
        copy.wait_send()
    for g in halves:
        for kind in range(4):
            g.first(kind).wait_send()
            for column in COLUMNS:
                g.second(column, kind).wait_send()


def body(qkv, tile_mask, d_out, w_out, momentum):
    worker_count = lax.axis_size("dp")
    tokens, head_size = qkv.shape[2], qkv.shape[4]
    width = d_out.shape[2]
    length = tokens * BLOCKS
    inv_root = 1.0 / math.sqrt(head_size)
    qkv_t = jnp.transpose(qkv[:, 0], (0, 2, 1, 3))
    vmem = pl.BlockSpec(memory_space=pltpu.VMEM)
    hbm = pl.BlockSpec(memory_space=pl.ANY)
    grads, weight_grad = pl.pallas_call(
        functools.partial(kernel, inv_root),
        out_shape=(
            jax.ShapeDtypeStruct((3, length, head_size), jnp.bfloat16),
            jax.ShapeDtypeStruct((head_size, width), jnp.float32),
        ),
        in_specs=[hbm, hbm, vmem, vmem],
        out_specs=(vmem, vmem),
        scratch_shapes=[
            pltpu.VMEM((3, length, head_size), jnp.bfloat16),
            pltpu.VMEM((BLOCKS, tokens, width), jnp.bfloat16),
            pltpu.VMEM((BLOCKS, length), jnp.float32),
            pltpu.VMEM((head_size, length), jnp.float32),
            pltpu.VMEM((head_size, length), jnp.float32),
            pltpu.SemaphoreType.DMA((BLOCKS - 1,)),
            pltpu.SemaphoreType.DMA((BLOCKS - 1,)),
            pltpu.SemaphoreType.DMA((40,)),
            pltpu.SemaphoreType.DMA((40,)),
            pltpu.SemaphoreType.DMA((2,)),
        ],
        compiler_params=pltpu.CompilerParams(
            collective_id=0, has_side_effects=True, vmem_limit_bytes=56 << 20
        ),
    )(qkv_t, d_out[0], w_out[0], tile_mask)
    head_grads = grads.reshape(3, 1, length, 1, head_size)
    grad_qkv = lax.all_to_all(head_grads, "seq", split_axis=2, concat_axis=3, tiled=True)
    worker_mom = 0.9 * momentum + 0.1 * weight_grad[None]
    worker_scale = jnp.mean(jnp.abs(worker_mom), axis=(1, 2), keepdims=True) + 1e-06
    sent = (worker_scale * jnp.tanh(worker_mom / worker_scale)).astype(jnp.bfloat16)
    worker_error = (worker_mom - sent.astype(jnp.float32))[None]
    received = lax.all_to_all(sent[None], "dp", split_axis=2, concat_axis=0, tiled=True)
    averaged = jnp.sum(received.astype(jnp.float32), axis=0) / worker_count
    server_scale = jnp.mean(jnp.abs(averaged), axis=(1, 2), keepdims=True) + 1e-06
    server_sent = (server_scale * jnp.tanh(averaged / server_scale)).astype(jnp.bfloat16)
    server_error = averaged - server_sent.astype(jnp.float32)
    synced_momentum = lax.all_gather(server_sent, "dp", axis=1, tiled=True)
    return (grad_qkv, synced_momentum, worker_error, server_error)


def solution(mesh):
    placed = (
        P(None, "dp", "seq", None, None),
        P(),
        P("dp", "seq", None),
        P("seq", None, None),
        P("seq", None, None),
    )
    return jax.shard_map(
        body,
        mesh=mesh,
        in_specs=placed,
        out_specs=(
            P(None, "dp", "seq", None, None),
            P("seq", None, None),
            P("dp", "seq", None, None),
            P("seq", "dp", None),
        ),
        check_vma=False,
    )
```

time: 306 us -> 174 us (0.57)
  the two profiles are of different devices: /device:TPU:49 before, /device:TPU:1 now
where the time goes in v1:
time: 174 us; the launch traced here: 173 us
  Pallas kernels  101 us (58%)
  local copies, waits for them, and re-layouts  26.2 us (15%)
  blocking collectives  14.5 us (8%)
  other arithmetic  12.3 us (7%)
  starting transfers between devices  10 us (6%)
  waiting for transfers between devices  7.25 us (4%)
  between operations  2.01 us (1%)
    pallas_call x1, Pallas kernels, body(): pl.pallas_call(functools.partial(kernel, inv_root), out_shape=(jax.ShapeD...  101 us
    all_gather x1, blocking collectives, body(): synced_momentum = lax.all_gather(server_sent, 'dp', axis=1, tiled=True)  14.5 us
    unnamed x12, local copies, waits for them, and re-layouts  11.8 us
    reshape x1, local copies, waits for them, and re-layouts, body(): head_grads = grads.reshape(3, 1, length, 1, head_size)  10.8 us
    all_to_all x1, starting transfers between devices, body(): lax.all_to_all(sent[None], 'dp', split_axis=2, concat_axis=0, tiled=True)  6.16 us
    all_to_all x1, waiting for transfers between devices, body(): lax.all_to_all(head_grads, 'seq', split_axis=2, concat_axis=3, tiled=True)  5.85 us
    unnamed x1, other arithmetic  5.35 us
    all_to_all x1, starting transfers between devices, body(): lax.all_to_all(head_grads, 'seq', split_axis=2, concat_axis=3, tiled=True)  3.86 us
  transfers between devices with their start and end apart: 2, of which 2 were waited for; matrix products, arithmetic and copies ran while one was open for 11% of the time, Pallas kernels for 0%

profile of v1, /device:TPU:1, one launch (start us, length us, event | category | flops | bytes accessed | tf_op | source)
XLA Modules:
  0.0 173.1 jit_solution(1628684763466925288)
XLA Ops:
  0.6 3.0 %copy.20 = bf16[3,1,128,16,128]{4,2,3,0,1:T(8,128)(2,1)} copy(bf16[3,1,128,16,128]{4,3,2,1,0:T(8,128)(2,1)} %param.5) | data formatting | bytes 3145728 | tf_op args[0]
  3.6 0.0 copy-start
  3.6 100.8 %shard_map.84 = (bf16[3,2048,128]{2,1,0:T(8,128)(2,1)}, f32[128,3072]{1,0:T(8,128)}) custom-call(bf16[3,16,128,128]{3,2,1,0:T(8,128)(2,1)} %bitcast.44, bf16[128,3072]{1,0:T(8,128)(2,1)} %bitcast.49, bf16[128,3072]{1,0:T(8,128)(2,1)} %bitcast.50, s32[8,16,16]{2,1,0:T(8,128)} %mask_ref.1), custom_call_target="tpu_custom_call" | custom-call | tf_op jit(solution)/shard_map/pallas_call | solution.py:269
  104.4 0.0 copy-done
  104.4 0.0 copy-start.1
  104.4 2.5 %abs_reduce_fusion = f32[]{:T(128)} fusion(f32[128,3072]{1,0:T(8,128)} %get-tuple-element.7, f32[1,128,3072]{2,1,0:T(8,128)S(1)} %copy-done), kind=kLoop, calls=%fused_computation.5 | loop fusion | flops 1966079 | bytes 3145732 | tf_op jit(solution)/shard_map/reduce_sum | solution.py:296
  107.6 0.0 copy-done.1
  107.6 1.5 subtract_bitcast_fusion
  109.2 1.2 copy.21
  110.4 0.5 broadcast.47
  110.9 5.4 %reduce.5 = bf16[128,3072]{1,0:T(8,128)(2,1)S(1)} reduce(bf16[128,1,1,3072]{3,2,1,0:T(2,128)(2,1)S(1)} %bitcast.43, bf16[]{:T(256)} %broadcast.47), dimensions={1,2}, to_apply=%bitcast.41.reduce_sub_computation | reduce | bytes 1572866
  116.3 0.0 copy-start.2
  116.3 1.5 reshape.91
  117.7 6.2 %all-to-all-start.1 = ((bf16[8,2,24576]{2,1,0:T(2,128)(2,1)}), bf16[8,2,24576]{2,1,0:T(2,128)(2,1)S(1)}, u32[]{:S(2)}, u32[]{:S(2)}) async-start(bf16[8,2,24576]{2,1,0:T(2,128)(2,1)} %reshape.91), calls=%async_computation.1 | async-start | bytes 1572864 | tf_op jit(solution)/shard_map/all_to_all | solution.py:299
  123.9 0.0 copy-done.2
  123.9 10.8 %copy.12 = bf16[3,1,2048,1,128]{4,0,3,1,2:T(4,128)(2,1)} copy(bf16[3,1,2048,1,128]{4,2,0,3,1:T(8,128)(2,1)S(1)} %bitcast.47) | data formatting | bytes 3145728 | tf_op jit(solution)/shard_map/reshape | solution.py:293
  134.7 1.4 all-to-all-done.1
  136.1 3.9 %all-to-all-start = ((bf16[3,1,2048,1,128]{4,0,3,1,2:T(4,128)(2,1)}), bf16[3,1,2048,1,128]{4,0,3,1,2:T(4,128)(2,1)S(1)}, u32[]{:S(2)}, u32[]{:S(2)}) async-start(bf16[3,1,2048,1,128]{4,0,3,1,2:T(4,128)(2,1)} %copy.12), calls=%async_computation | async-start | bytes 4194304 | tf_op jit(solution)/shard_map/all_to_all | solution.py:294
  139.9 3.2 %reshape.92 = bf16[128,1,1,3072]{3,2,1,0:T(2,128)(2,1)} reshape(bf16[8,2,24576]{2,1,0:T(2,128)(2,1)S(1)} %all-to-all-done.1) | data formatting | bytes 1572864
  143.1 2.8 %copy.15 = f32[1,1,128,3072]{3,2,0,1:T(8,128)} copy(bf16[1,1,128,3072]{3,1,0,2:T(2,128)(2,1)} %bitcast.46) | data formatting | bytes 2359296
  146.0 1.5 reduce_sum.28
  147.5 0.7 abs_reduce_fusion.1
  148.8 0.7 bitcast_subtract_fusion
  149.5 14.5 %all_gather.3 = bf16[1,128,3072]{2,1,0:T(8,128)(2,1)S(1)} all-gather(bf16[1,16,3072]{2,1,0:T(8,128)(2,1)S(1)} %get-tuple-element.11), channel_id=1, replica_groups=mesh['dp'=8,'seq'=16] {'dp'}, dimensions={1}, use_global_device_ids=true | all-gather | bytes 884736 | tf_op jit(solution)/shard_map/all_gather | solution.py:304
  164.0 5.8 %all-to-all-done = bf16[3,1,2048,1,128]{4,0,3,1,2:T(4,128)(2,1)S(1)} async-done(((bf16[3,1,2048,1,128]{4,0,3,1,2:T(4,128)(2,1)}), bf16[3,1,2048,1,128]{4,0,3,1,2:T(4,128)(2,1)S(1)}, u32[]{:S(2)}, u32[]{:S(2)}) %all-to-all-start) | async-done | bytes 1572896 | tf_op jit(solution)/shard_map/all_to_all | solution.py:294
  169.8 2.4 %copy.19 = bf16[3,1,16,128,1,128]{5,2,3,0,4,1:T(8,128)(2,1)} copy(bf16[3,1,16,128,1,128]{5,0,3,2,4,1:T(4,128)(2,1)S(1)} %bitcast.42) | data formatting | bytes 3145728 | tf_op jit(solution)/shard_map/all_to_all | solution.py:294
  172.2 0.9 copy.23
Async XLA Ops:
  3.6 100.8 %copy-start = (f32[1,128,3072]{2,1,0:T(8,128)S(1)}, f32[1,128,3072]{2,1,0:T(8,128)}, u32[]{:S(2)}) copy-start(f32[1,128,3072]{2,1,0:T(8,128)} %param.9) | copy-start | bytes 4718596
  104.4 3.2 %copy-start.1 = (f32[128,3072]{1,0:T(8,128)S(1)}, f32[128,3072]{1,0:T(8,128)}, u32[]{:S(2)}) copy-start(f32[128,3072]{1,0:T(8,128)} %get-tuple-element.7) | copy-start | bytes 4718596
  116.3 7.6 %copy-start.2 = (bf16[3,2048,128]{2,1,0:T(8,128)(2,1)S(1)}, bf16[3,2048,128]{2,1,0:T(8,128)(2,1)}, u32[]{:S(2)}) copy-start(bf16[3,2048,128]{2,1,0:T(8,128)(2,1)} %get-tuple-element.6) | copy-start | bytes 4718596
  117.7 18.3 %all-to-all-start.1 = ((bf16[8,2,24576]{2,1,0:T(2,128)(2,1)}), bf16[8,2,24576]{2,1,0:T(2,128)(2,1)S(1)}, u32[]{:S(2)}, u32[]{:S(2)}) async-start(bf16[8,2,24576]{2,1,0:T(2,128)(2,1)} %reshape.91), calls=%async_computation.1 | async-start | bytes 1572864 | tf_op jit(solution)/shard_map/all_to_all | solution.py:299
  136.1 33.8 %all-to-all-start = ((bf16[3,1,2048,1,128]{4,0,3,1,2:T(4,128)(2,1)}), bf16[3,1,2048,1,128]{4,0,3,1,2:T(4,128)(2,1)S(1)}, u32[]{:S(2)}, u32[]{:S(2)}) async-start(bf16[3,1,2048,1,128]{4,0,3,1,2:T(4,128)(2,1)} %copy.12), calls=%async_computation | async-start | bytes 4194304 | tf_op jit(solution)/shard_map/all_to_all | solution.py:294

commit v2 on v1

--- a/solution.py
+++ b/solution.py
@@ -13,6 +13,7 @@
 TILE = 128
 SIDE = 4
 BLOCKS = SIDE * SIDE
+WORKERS = 8
 HALF = TILE // 2
 MESH = pl.DeviceIdType.MESH
 
@@ -96,21 +97,28 @@
 
 def kernel(
     inv_root,
-    qkv_ref, dout_ref, w_ref, mask_ref,
-    grads_ref, gw_ref,
-    qkvbuf, dbuf, bias, dkt, dvt,
-    q_send, q_recv, d_send, d_recv, local_sem,
+    qkv_ref, dout_ref, w_hbm, mask_ref, mom_hbm,
+    grads_ref, sync_ref, werr_ref, serr_ref,
+    qkvbuf, dbuf, w_ref, mom_ref, bias, dqbuf, dkt, dvt, kvbuf, gw_ref,
+    sentbuf, werrbuf, landed, syncbuf, serrbuf,
+    q_send, q_recv, d_send, d_recv, g_send, g_recv, kv_send, kv_recv,
+    m_send, m_recv, s_send, s_recv, local_sem,
 ):
     me = lax.axis_index("seq")
     z = me // SIDE
     y = lax.rem(me, SIDE)
+    worker = lax.axis_index("dp")
+    x = worker // 2
+    core = lax.rem(worker, 2)
+    width = dout_ref.shape[1]
+    rows = sentbuf.shape[0] // WORKERS
     peers = [
         wrap(z, dz) * SIDE + wrap(y, dy)
         for dz in range(SIDE) for dy in range(SIDE) if (dz, dy) != (0, 0)
     ]
-    sources = [
-        wrap(z, -dz) * SIDE + wrap(y, -dy)
-        for dz in range(SIDE) for dy in range(SIDE) if (dz, dy) != (0, 0)
+    workers = [
+        wrap(x, dx) * 2 + lax.rem(core + dc, 2)
+        for dx in (2, 1, -1, 0) for dc in range(2) if (dx, dc) != (0, 0)
     ]
 
     own_d = pltpu.make_async_copy(dout_ref, dbuf.at[me], local_sem.at[0])
@@ -119,11 +127,17 @@
         qkv_ref.at[:, me], qkvbuf.at[:, pl.ds(me * TILE, TILE)], local_sem.at[1]
     )
     own_q.start()
+    own_w = pltpu.make_async_copy(w_hbm, w_ref, local_sem.at[2])
+    own_w.start()
+    own_m = pltpu.make_async_copy(mom_hbm, mom_ref, local_sem.at[3])
+    own_m.start()
 
     barrier = pltpu.get_barrier_semaphore()
     for peer in peers:
         pl.semaphore_signal(barrier, inc=1, device_id={"seq": peer}, device_id_type=MESH)
-    pl.semaphore_wait(barrier, len(peers))
+    for peer in workers:
+        pl.semaphore_signal(barrier, inc=1, device_id={"dp": peer}, device_id_type=MESH)
+    pl.semaphore_wait(barrier, len(peers) + len(workers))
 
     q_copies = []
     for index, peer in enumerate(peers):
@@ -161,7 +175,9 @@
     gw_ref[...] = jnp.zeros_like(gw_ref)
 
     own_q.wait()
-    for index, copy in enumerate(q_copies):
+    own_w.wait()
+    own_m.wait()
+    for copy in q_copies:
         copy.wait_recv()
 
     def arrive(step):
@@ -213,15 +229,28 @@
                 g.second(2, 2).wait_recv()
                 g.second(2, 3).wait_recv()
 
+    def dq_copy(step, block):
+        return pltpu.make_async_remote_copy(
+            src_ref=dqbuf.at[pl.ds(pl.multiple_of(block * TILE, TILE), TILE)],
+            dst_ref=grads_ref.at[0, me],
+            send_sem=g_send.at[step],
+            recv_sem=g_recv.at[step],
+            device_id={"seq": block},
+            device_id_type=MESH,
+        )
+
+    def block_of(step):
+        return wrap(z, pick(step, [o[0] for o in ORDER])) * SIDE + wrap(
+            y, pick(step, [o[1] for o in ORDER])
+        )
+
     def body(step, carry):
         for number in (1, 2, 5, 9, 11, 15):
             @pl.when(step == number)
             def _():
                 arrive(number)
 
-        block = wrap(z, pick(step, [o[0] for o in ORDER])) * SIDE + wrap(
-            y, pick(step, [o[1] for o in ORDER])
-        )
+        block = block_of(step)
         row0 = pl.multiple_of(block * TILE, TILE)
         q = qkvbuf[0, pl.ds(row0, TILE), :]
         k = qkvbuf[1]
@@ -238,15 +267,104 @@
             cot.astype(jnp.float32) * att.astype(jnp.float32), axis=-1, keepdims=True
         )
         dscores = (probs * (nt(cot, v) - delta)).astype(jnp.bfloat16)
-        grads_ref[0, pl.ds(row0, TILE), :] = (nn(dscores, k) * inv_root).astype(jnp.bfloat16)
+        dqbuf[pl.ds(row0, TILE), :] = (nn(dscores, k) * inv_root).astype(jnp.bfloat16)
+
+        @pl.when(step > 0)
+        def _():
+            dq_copy(step, block).start()
+
         dkt[...] += tn(q, dscores)
         dvt[...] += tn(cot, probs_b)
         gw_ref[...] += tn(att, d)
         return carry
 
     lax.fori_loop(0, BLOCKS, body, 0)
-    grads_ref[1] = (dkt[...].T * inv_root).astype(jnp.bfloat16)
-    grads_ref[2] = dvt[...].T.astype(jnp.bfloat16)
+
+    def moment(index, total):
+        at = pl.ds(pl.multiple_of(index * rows, rows), rows)
+        value = 0.9 * mom_ref[at, :] + 0.1 * gw_ref[at, :]
+        mom_ref[at, :] = value
+        return total + jnp.abs(value)
+
+    total = lax.fori_loop(0, WORKERS, moment, jnp.zeros((rows, width), jnp.float32))
+    scale = jnp.sum(total, axis=(0, 1), keepdims=True) / (rows * WORKERS * width) + 1e-06
+    unscale = 1.0 / scale
+
+    def compress(index, carry):
+        at = pl.ds(pl.multiple_of(index * rows, rows), rows)
+        value = mom_ref[at, :]
+        code = (scale * jnp.tanh(value * unscale)).astype(jnp.bfloat16)
+        sentbuf[at, :] = code
+        werrbuf[at, :] = value - code.astype(jnp.float32)
+        return carry
+
+    lax.fori_loop(0, WORKERS, compress, 0)
+    m_copies = []
+    for index, peer in enumerate(workers):
+        copy = pltpu.make_async_remote_copy(
+            src_ref=sentbuf.at[pl.ds(pl.multiple_of(peer * rows, rows), rows)],
+            dst_ref=landed.at[worker],
+            send_sem=m_send.at[index],
+            recv_sem=m_recv.at[index],
+            device_id={"dp": peer},
+            device_id_type=MESH,
+        )
+        copy.start()
+        m_copies.append(copy)
+    landed[worker] = sentbuf[pl.ds(pl.multiple_of(worker * rows, rows), rows), :]
+    werr_out = pltpu.make_async_copy(werrbuf, werr_ref, local_sem.at[4])
+    werr_out.start()
+
+    kvbuf[0] = (dkt[...].T * inv_root).astype(jnp.bfloat16)
+    kvbuf[1] = dvt[...].T.astype(jnp.bfloat16)
+    kv_copies = []
+    for index, peer in enumerate(peers):
+        copy = pltpu.make_async_remote_copy(
+            src_ref=kvbuf.at[:, pl.ds(peer * TILE, TILE)],
+            dst_ref=grads_ref.at[pl.ds(1, 2), me],
+            send_sem=kv_send.at[index],
+            recv_sem=kv_recv.at[index],
+            device_id={"seq": peer},
+            device_id_type=MESH,
+        )
+        copy.start()
+        kv_copies.append(copy)
+    own_kv = pltpu.make_async_copy(
+        kvbuf.at[:, pl.ds(me * TILE, TILE)], grads_ref.at[pl.ds(1, 2), me], local_sem.at[5]
+    )
+    own_kv.start()
+    own_dq = pltpu.make_async_copy(
+        dqbuf.at[pl.ds(me * TILE, TILE)], grads_ref.at[0, me], local_sem.at[6]
+    )
+    own_dq.start()
+
+    for copy in m_copies:
+        copy.wait_recv()
+    average = landed[0].astype(jnp.float32)
+    for index in range(1, WORKERS):
+        average = average + landed[index].astype(jnp.float32)
+    average = average / WORKERS
+    server = jnp.sum(jnp.abs(average), axis=(0, 1), keepdims=True) / (rows * width) + 1e-06
+    code = (server * jnp.tanh(average * (1.0 / server))).astype(jnp.bfloat16)
+    syncbuf[...] = code
+    serrbuf[...] = average - code.astype(jnp.float32)
+    mine = sync_ref.at[pl.ds(pl.multiple_of(worker * rows, rows), rows)]
+    s_copies = []
+    for index, peer in enumerate(workers):
+        copy = pltpu.make_async_remote_copy(
+            src_ref=syncbuf,
+            dst_ref=mine,
+            send_sem=s_send.at[index],
+            recv_sem=s_recv.at[index],
+            device_id={"dp": peer},
+            device_id_type=MESH,
+        )
+        copy.start()
+        s_copies.append(copy)
+    own_s = pltpu.make_async_copy(syncbuf, mine, local_sem.at[7])
+    own_s.start()
+    serr_out = pltpu.make_async_copy(serrbuf, serr_ref, local_sem.at[8])
+    serr_out.start()
 
     for copy in q_copies:
         copy.wait_send()
@@ -255,54 +373,70 @@
             g.first(kind).wait_send()
             for column in COLUMNS:
                 g.second(column, kind).wait_send()
+    for copy in m_copies:
+        copy.wait_send()
+
+    def drain(step, carry):
+        dq_copy(step, block_of(step)).wait()
+        return carry
+
+    lax.fori_loop(1, BLOCKS, drain, 0)
+    for copy in kv_copies + s_copies:
+        copy.wait()
+    for copy in (own_kv, own_dq, own_s, werr_out, serr_out):
+        copy.wait()
 
 
 def body(qkv, tile_mask, d_out, w_out, momentum):
-    worker_count = lax.axis_size("dp")
     tokens, head_size = qkv.shape[2], qkv.shape[4]
     width = d_out.shape[2]
     length = tokens * BLOCKS
     inv_root = 1.0 / math.sqrt(head_size)
+    rows = head_size // WORKERS
     qkv_t = jnp.transpose(qkv[:, 0], (0, 2, 1, 3))
     vmem = pl.BlockSpec(memory_space=pltpu.VMEM)
     hbm = pl.BlockSpec(memory_space=pl.ANY)
-    grads, weight_grad = pl.pallas_call(
+    dma = pltpu.SemaphoreType.DMA
+    grads, synced, worker_error, server_error = pl.pallas_call(
         functools.partial(kernel, inv_root),
         out_shape=(
-            jax.ShapeDtypeStruct((3, length, head_size), jnp.bfloat16),
+            jax.ShapeDtypeStruct((3, HEADS, tokens, head_size), jnp.bfloat16),
+            jax.ShapeDtypeStruct((head_size, width), jnp.bfloat16),
             jax.ShapeDtypeStruct((head_size, width), jnp.float32),
+            jax.ShapeDtypeStruct((rows, width), jnp.float32),
         ),
-        in_specs=[hbm, hbm, vmem, vmem],
-        out_specs=(vmem, vmem),
+        in_specs=[hbm, hbm, hbm, vmem, hbm],
+        out_specs=(hbm, hbm, hbm, hbm),
         scratch_shapes=[
             pltpu.VMEM((3, length, head_size), jnp.bfloat16),
             pltpu.VMEM((BLOCKS, tokens, width), jnp.bfloat16),
+            pltpu.VMEM((head_size, width), jnp.bfloat16),
+            pltpu.VMEM((head_size, width), jnp.float32),
             pltpu.VMEM((BLOCKS, length), jnp.float32),
+            pltpu.VMEM((length, head_size), jnp.bfloat16),
             pltpu.VMEM((head_size, length), jnp.float32),
             pltpu.VMEM((head_size, length), jnp.float32),
-            pltpu.SemaphoreType.DMA((BLOCKS - 1,)),
-            pltpu.SemaphoreType.DMA((BLOCKS - 1,)),
-            pltpu.SemaphoreType.DMA((40,)),
-            pltpu.SemaphoreType.DMA((40,)),
-            pltpu.SemaphoreType.DMA((2,)),
+            pltpu.VMEM((2, length, head_size), jnp.bfloat16),
+            pltpu.VMEM((head_size, width), jnp.float32),
+            pltpu.VMEM((head_size, width), jnp.bfloat16),
+            pltpu.VMEM((head_size, width), jnp.float32),
+            pltpu.VMEM((WORKERS, rows, width), jnp.bfloat16),
+            pltpu.VMEM((rows, width), jnp.bfloat16),
+            pltpu.VMEM((rows, width), jnp.float32),
+            dma((BLOCKS - 1,)), dma((BLOCKS - 1,)),
+            dma((40,)), dma((40,)),
+            dma((BLOCKS,)), dma((BLOCKS,)),
+            dma((BLOCKS - 1,)), dma((BLOCKS - 1,)),
+            dma((WORKERS - 1,)), dma((WORKERS - 1,)),
+            dma((WORKERS - 1,)), dma((WORKERS - 1,)),
+            dma((9,)),
         ],
         compiler_params=pltpu.CompilerParams(
             collective_id=0, has_side_effects=True, vmem_limit_bytes=56 << 20
         ),
-    )(qkv_t, d_out[0], w_out[0], tile_mask)
-    head_grads = grads.reshape(3, 1, length, 1, head_size)
-    grad_qkv = lax.all_to_all(head_grads, "seq", split_axis=2, concat_axis=3, tiled=True)
-    worker_mom = 0.9 * momentum + 0.1 * weight_grad[None]
-    worker_scale = jnp.mean(jnp.abs(worker_mom), axis=(1, 2), keepdims=True) + 1e-06
-    sent = (worker_scale * jnp.tanh(worker_mom / worker_scale)).astype(jnp.bfloat16)
-    worker_error = (worker_mom - sent.astype(jnp.float32))[None]
-    received = lax.all_to_all(sent[None], "dp", split_axis=2, concat_axis=0, tiled=True)
-    averaged = jnp.sum(received.astype(jnp.float32), axis=0) / worker_count
-    server_scale = jnp.mean(jnp.abs(averaged), axis=(1, 2), keepdims=True) + 1e-06
-    server_sent = (server_scale * jnp.tanh(averaged / server_scale)).astype(jnp.bfloat16)
-    server_error = averaged - server_sent.astype(jnp.float32)
-    synced_momentum = lax.all_gather(server_sent, "dp", axis=1, tiled=True)
-    return (grad_qkv, synced_momentum, worker_error, server_error)
+    )(qkv_t, d_out[0], w_out[0], tile_mask, momentum[0])
+    grad_qkv = jnp.transpose(grads, (0, 2, 1, 3))[:, None]
+    return (grad_qkv, synced[None], worker_error[None, None], server_error[None])
 
 
 def solution(mesh):

time: 174 us -> 134 us (0.77)
  Pallas kernels: 101 us -> 123 us
  local copies, waits for them, and re-layouts: 26.2 us -> 10.1 us
  blocking collectives: 14.5 us -> 0 us
  other arithmetic: 12.3 us -> 0 us
  starting transfers between devices: 10 us -> 0 us
  waiting for transfers between devices: 7.25 us -> 0 us
    pallas_call x1, Pallas kernels: 101 us -> 123 us  [body(): pl.pallas_call(functools.partial(kernel, inv_root), out_shape=(jax.ShapeD...]
    all_gather x1 -> x0, blocking collectives: 14.5 us -> none  [body(): synced_momentum = lax.all_gather(server_sent, 'dp', axis=1, tiled=True)]
    reshape x1 -> x0, local copies, waits for them, and re-layouts: 10.8 us -> none  [body(): head_grads = grads.reshape(3, 1, length, 1, head_size)]
    all_to_all x2 -> x0, starting transfers between devices: 10 us -> none  [the longest x1 6.16 us: body(): lax.all_to_all(sent[None], 'dp', split_axis=2, concat_axis=0, tiled=True)]
    all_to_all x2 -> x0, waiting for transfers between devices: 7.25 us -> none  [the longest x1 5.85 us: body(): lax.all_to_all(head_grads, 'seq', split_axis=2, concat_axis=3, tiled=True)]
    unnamed x1 -> x0, other arithmetic: 5.35 us -> none
    reduce_sum x3 -> x0, other arithmetic: 4.69 us -> none  [the longest x1 2.54 us: body(): jnp.mean(jnp.abs(worker_mom), axis=(1, 2), keepdims=True) + 1e-06]
    all_to_all x1 -> x0, local copies, waits for them, and re-layouts: 2.43 us -> none  [body(): lax.all_to_all(head_grads, 'seq', split_axis=2, concat_axis=3, tiled=True)]
  transfers between devices with their start and end apart: 2 -> 0, of which waited for: 2 -> 0; matrix products, arithmetic and copies ran while one was open for 11% -> 0% of each run, Pallas kernels for 0% -> 0%
where the time goes in v2:
time: 134 us
  Pallas kernels  123 us (92%)
  local copies, waits for them, and re-layouts  10.1 us (8%)
    pallas_call x1, Pallas kernels, body(): pl.pallas_call(functools.partial(kernel, inv_root), out_shape=(jax.ShapeD...  123 us
    unnamed x11, local copies, waits for them, and re-layouts  10.1 us

profile of v2, /device:TPU:1, one launch (start us, length us, event | category | flops | bytes accessed | tf_op | source)
XLA Modules:
  0.0 133.6 jit_solution(16516303530337018174)
XLA Ops:
  0.6 3.0 %copy.12 = bf16[3,1,128,16,128]{4,2,3,0,1:T(8,128)(2,1)} copy(bf16[3,1,128,16,128]{4,3,2,1,0:T(8,128)(2,1)} %param.5) | data formatting | bytes 3145728 | tf_op args[0]
  3.6 122.9 %shard_map.84 = (bf16[3,16,128,128]{3,2,1,0:T(8,128)(2,1)}, bf16[128,3072]{1,0:T(8,128)(2,1)}, f32[128,3072]{1,0:T(8,128)}, f32[16,3072]{1,0:T(8,128)}) custom-call(bf16[3,16,128,128]{3,2,1,0:T(8,128)(2,1)} %bitcast.14, bf16[128,3072]{1,0:T(8,128)(2,1)} %bitcast.18, bf16[128,3072]{1,0:T(8,128)(2,1)} %bitcast.19, s32[8,16,16]{2,1,0:T(8,128)} %mask_ref.1, ...), custom_call_target="tpu_custom_call" | custom-call | tf_op jit(solution)/shard_map/pallas_call | solution.py:400
  126.5 0.0 copy-start.1
  126.5 3.6 %copy.10 = bf16[3,1,128,16,128]{4,3,2,1,0:T(8,128)(2,1)} copy(bf16[3,1,128,16,128]{4,2,3,0,1:T(8,128)(2,1)} %bitcast.16) | data formatting | bytes 3145728
  130.1 0.0 copy-start
  130.1 0.0 copy-done.1
  130.1 0.9 copy.16
  131.0 0.8 copy-done
  131.8 0.0 copy-start.2
  131.8 1.1 copy.17
  133.0 0.0 copy-done.2
  133.0 0.7 copy.18
Async XLA Ops:
  126.5 3.7 %copy-start.1 = (bf16[128,3072]{1,0:T(8,128)(2,1)S(1)}, bf16[128,3072]{1,0:T(8,128)(2,1)}, u32[]{:S(2)}) copy-start(bf16[128,3072]{1,0:T(8,128)(2,1)} %get-tuple-element.9) | copy-start | bytes 2359300
  130.1 1.7 %copy-start = (f32[128,3072]{1,0:T(8,128)S(1)}, f32[128,3072]{1,0:T(8,128)}, u32[]{:S(2)}) copy-start(f32[128,3072]{1,0:T(8,128)} %get-tuple-element.10) | copy-start | bytes 4718596
  131.8 1.1 copy-start.2

commit v3 on v2

v3 whole, which is shorter than its diff:
```python
import functools
import math

import jax
import jax.numpy as jnp
from jax import lax
from jax.experimental import pallas as pl
from jax.experimental.pallas import tpu as pltpu
from jax.sharding import PartitionSpec as P

HEADS = 16
GROUPS = 8
TILE = 128
SIDE = 4
BLOCKS = SIDE * SIDE
WORKERS = 8
HALF = TILE // 2
PART = HALF // 2
MESH = pl.DeviceIdType.MESH

ORDER = (
    (0, 0), (0, 1), (0, 2), (0, 3),
    (-1, 0), (-1, 1), (1, 0), (1, 1),
    (2, 0), (2, 1),
    (-1, 2), (-1, 3), (1, 2), (1, 3),
    (2, 2), (2, 3),
)
OFFSETS = (0, -1, 1, 2)


def wrap(position, offset):
    return lax.rem(position + (offset + SIDE), SIDE)


def pick(step, table):
    value = jnp.int32(table[0])
    for index, entry in enumerate(table):
        if index and entry != table[0]:
            value = jnp.where(step == index, jnp.int32(entry), value)
    return value


def nt(a, b):
    return lax.dot_general(a, b, (((1,), (1,)), ((), ())), preferred_element_type=jnp.float32)


def nn(a, b):
    return lax.dot_general(a, b, (((1,), (0,)), ((), ())), preferred_element_type=jnp.float32)


def tn(a, b):
    return lax.dot_general(a, b, (((0,), (0,)), ((), ())), preferred_element_type=jnp.float32)


class Gather:
    def __init__(self, buf, z, columns, row0, send, recv):
        self.buf, self.z, self.columns, self.row0 = buf, z, columns, row0
        self.send, self.recv = send, recv

    def block(self, dz, column):
        return wrap(self.z, dz) * SIDE + self.columns[column]

    def copy(self, slot, block, lo, n, dz, column):
        rows = self.buf.at[block, pl.ds(pl.multiple_of(self.row0 + lo, PART // 2), n)]
        return pltpu.make_async_remote_copy(
            src_ref=rows,
            dst_ref=rows,
            send_sem=self.send.at[slot],
            recv_sem=self.recv.at[slot],
            device_id={"seq": self.block(dz, column)},
            device_id_type=MESH,
        )

    def ring(self, slot, column, kind, lo):
        if kind == 0:
            return self.copy(slot, self.block(0, column), lo, PART, 1, 0)
        if kind == 1:
            return self.copy(slot, self.block(0, column), lo, PART, -1, 0)
        if kind == 2:
            return self.copy(slot, self.block(-1, column), lo, PART // 2, 1, 0)
        return self.copy(slot, self.block(1, column), lo + PART // 2, PART // 2, -1, 0)

    def az(self, column, kind):
        return self.ring(column * 4 + kind, column, kind, 0)

    def ay(self, dz, column):
        slot = 8 + OFFSETS.index(dz) * 2 + column
        return self.copy(slot, self.block(dz, column), 0, PART, 0, 2)

    def by(self, column):
        return self.copy(16 + column, self.block(0, column), PART, PART, 0, 2)

    def bz(self, column, kind):
        return self.ring(18 + column * 4 + kind, column, kind, PART)

    def every(self):
        copies = [self.az(c, kind) for c in range(2) for kind in range(4)]
        copies += [self.ay(dz, c) for dz in OFFSETS for c in range(2)]
        copies += [self.by(c) for c in range(2)]
        return copies + [self.bz(c, kind) for c in range(4) for kind in range(4)]


def kernel(
    inv_root,
    qkv_ref, dout_ref, w_hbm, mask_ref, mom_hbm,
    grads_ref, sync_ref, werr_ref, serr_ref,
    qkvbuf, dbuf, w_ref, mom_ref, bias, dqbuf, dkt, dvt, kvbuf, gw_ref,
    sentbuf, werrbuf, landed, syncbuf, serrbuf, gwout, gwin,
    q_send, q_recv, d_send, d_recv, f_send, f_recv, i_send, i_recv,
    g_send, g_recv, kv_send, kv_recv, x_send, x_recv,
    m_send, m_recv, s_send, s_recv, local_sem,
):
    me = lax.axis_index("seq")
    z = me // SIDE
    y = lax.rem(me, SIDE)
    worker = lax.axis_index("dp")
    x = worker // 2
    core = lax.rem(worker, 2)
    width = dout_ref.shape[1]
    rows = sentbuf.shape[0] // WORKERS

    side = y // 2
    home = core == side
    away = core != side
    columns = (y, 3 - y, y + 1 - 2 * lax.rem(y, 2), 2 - y + 2 * lax.rem(y, 2))
    other = x * 2 + 1 - core
    partner = z * SIDE + 3 - y
    head = jnp.where(home, me, partner)
    swap = {"dp": other, "seq": partner}
    slot_of_job = lax.rem(y, 2) * 2 + core

    own_d = pltpu.make_async_copy(dout_ref, dbuf.at[me], local_sem.at[0])
    own_q = pltpu.make_async_copy(
        qkv_ref.at[:, me], qkvbuf.at[:, pl.ds(me * TILE, TILE)], local_sem.at[1]
    )
    own_w = pltpu.make_async_copy(w_hbm, w_ref, local_sem.at[2])
    own_m = pltpu.make_async_copy(mom_hbm, mom_ref, local_sem.at[3])

    @pl.when(home)
    def _():
        own_d.start()
        own_q.start()
        own_w.start()

    own_m.start()

    workers = [
        wrap(x, dx) * 2 + lax.rem(core + dc, 2)
        for dx in (2, 1, -1, 0) for dc in range(2) if (dx, dc) != (0, 0)
    ]
    plane = [
        (x * 2 + lax.rem(core + dc, 2), wrap(z, dz) * SIDE + wrap(y, dy))
        for dc in range(2) for dz in range(SIDE) for dy in range(SIDE) if (dc, dz, dy) != (0, 0, 0)
    ]
    barrier = pltpu.get_barrier_semaphore()
    for dp, seq in plane:
        pl.semaphore_signal(
            barrier, inc=1, device_id={"dp": dp, "seq": seq}, device_id_type=MESH
        )
    for peer in workers[:-1]:
        pl.semaphore_signal(barrier, inc=1, device_id={"dp": peer}, device_id_type=MESH)
    pl.semaphore_wait(barrier, len(plane) + len(workers) - 1)

    starts = []
    for h in range(2):
        at = pl.ds(h * HALF, HALF)
        copy = pltpu.make_async_remote_copy(
            src_ref=dout_ref.at[at],
            dst_ref=dbuf.at[me, at],
            send_sem=i_send.at[h],
            recv_sem=i_recv.at[jnp.where(home, h, 2)],
            device_id={
                "dp": jnp.where(home, other, x * 2 + h),
                "seq": jnp.where(home, me, partner),
            },
            device_id_type=MESH,
        )
        copy.start()
        starts.append(copy)

    def landing(slot):
        at = pl.ds(0, HALF)
        return pltpu.make_async_remote_copy(
            src_ref=dout_ref.at[at],
            dst_ref=dbuf.at[me, at],
            send_sem=i_send.at[0],
            recv_sem=i_recv.at[slot],
            device_id=swap,
            device_id_type=MESH,
        )

    w_copy = pltpu.make_async_remote_copy(
        src_ref=w_hbm, dst_ref=w_ref, send_sem=x_send.at[0], recv_sem=x_recv.at[0],
        device_id=swap, device_id_type=MESH,
    )
    pl.when(away)(w_copy.start)

    def q_copy(dz, u, c, recv):
        z2, y2 = wrap(z, dz), 2 * core + u
        theirs = z2 * SIDE + jnp.where(core == c, y2, 3 - y2)
        return pltpu.make_async_remote_copy(
            src_ref=qkv_ref.at[:, theirs],
            dst_ref=qkvbuf.at[:, pl.ds(me * TILE, TILE)],
            send_sem=q_send.at[dz * 4 + u * 2 + c],
            recv_sem=q_recv.at[recv],
            device_id={"dp": x * 2 + c, "seq": z2 * SIDE + y2},
            device_id_type=MESH,
        )

    def q_mine(dz, u, c):
        return (2 * core + u == y) & (core == c) if dz == 0 else None

    def unless(mine, action):
        if mine is None:
            action()
        else:
            pl.when(jnp.logical_not(mine))(action)

    q_keys = [(dz, u, c) for dz in range(SIDE) for u in range(2) for c in range(2)]
    for key in q_keys:
        unless(q_mine(*key), q_copy(*key, key[0] * 4 + y).start)

    gather = Gather(dbuf, z, columns, core * HALF, d_send, d_recv)

    def launch(column):
        gather.by(column).start()
        gather.az(column, 0).start()
        gather.az(column, 1).start()
        gather.ay(0, column).start()
        gather.bz(column, 0).start()
        gather.bz(column, 1).start()

    def block_of(step):
        column = pick(step, [o[1] for o in ORDER])
        base = jnp.where(column < 2, columns[0], columns[2])
        return wrap(z, pick(step, [o[0] for o in ORDER])) * SIDE + jnp.where(
            lax.rem(column, 2) == 0, base, 3 - base
        )

    def forward(step, block):
        at = dbuf.at[block, pl.ds(pl.multiple_of(core * HALF, HALF), HALF)]
        return pltpu.make_async_remote_copy(
            src_ref=at, dst_ref=at, send_sem=f_send.at[step], recv_sem=f_recv.at[step],
            device_id={"dp": other}, device_id_type=MESH,
        )

    def pass_on(dz, column):
        forward(ORDER.index((dz, column)), gather.block(dz, column)).start()

    pl.when(home)(own_d.wait)
    pl.when(away)(landing(core).wait_recv)
    launch(0)
    landing(2).wait_recv()
    launch(1)
    pass_on(0, 1)

    tiles = mask_ref[head // (HEADS // GROUPS)]
    for j in range(BLOCKS):
        bias[:, j * TILE:(j + 1) * TILE] = jnp.broadcast_to(
            jnp.where(tiles[:, j:j + 1] > 0, 0.0, -jnp.inf), (BLOCKS, TILE)
        )
    dkt[...] = jnp.zeros_like(dkt)
    dvt[...] = jnp.zeros_like(dvt)
    gw_ref[...] = jnp.zeros_like(gw_ref)

    for column in range(2):
        gather.az(column, 0).wait_recv()
        gather.az(column, 2).start()
        gather.ay(-1, column).start()
        gather.az(column, 1).wait_recv()
        gather.az(column, 3).start()
        gather.ay(1, column).start()
    for column in range(2):
        gather.by(column).wait_recv()
        gather.bz(column + 2, 0).start()
        gather.bz(column + 2, 1).start()

    own_m.wait()
    pl.when(away)(landing(1 - core).wait_recv)
    pl.when(home)(own_q.wait)
    pl.when(home)(own_w.wait)
    pl.when(away)(w_copy.wait_recv)
    for dz in range(SIDE):
        for source in range(SIDE):
            unless((y == source) & home if dz == 0 else None,
                   q_copy(dz, 0, 0, dz * 4 + source).wait_recv)

    def arrive(step):
        if step == 2:
            for column in range(2):
                gather.ay(0, column).wait_recv()
                pass_on(0, column + 2)
        elif step == 4:
            for column in range(2):
                gather.az(column, 2).wait_recv()
                gather.az(column, 3).wait_recv()
                gather.ay(2, column).start()
            for column in range(2):
                gather.bz(column, 0).wait_recv()
                gather.bz(column, 2).start()
                pass_on(-1, column)
                gather.bz(column, 1).wait_recv()
                gather.bz(column, 3).start()
                pass_on(1, column)
        elif step == 8:
            for column in range(2):
                gather.bz(column, 2).wait_recv()
                gather.bz(column, 3).wait_recv()
                pass_on(2, column)
            for column in range(2, 4):
                gather.bz(column, 0).wait_recv()
                gather.bz(column, 2).start()
                gather.bz(column, 1).wait_recv()
                gather.bz(column, 3).start()
        elif step == 10:
            for column in range(2):
                gather.ay(-1, column).wait_recv()
                pass_on(-1, column + 2)
        elif step == 12:
            for column in range(2):
                gather.ay(1, column).wait_recv()
                pass_on(1, column + 2)
        elif step == 14:
            for column in range(2):
                gather.bz(column + 2, 2).wait_recv()
                gather.bz(column + 2, 3).wait_recv()
                gather.ay(2, column).wait_recv()
                pass_on(2, column + 2)

    def dq_copy(step, block, recv):
        return pltpu.make_async_remote_copy(
            src_ref=dqbuf.at[pl.ds(pl.multiple_of(block * TILE, TILE), TILE)],
            dst_ref=grads_ref.at[0, head],
            send_sem=g_send.at[step],
            recv_sem=g_recv.at[recv],
            device_id={"dp": x * 2 + side, "seq": block},
            device_id_type=MESH,
        )

    def body(step, carry):
        for number in (2, 4, 8, 10, 12, 14):
            @pl.when(step == number)
            def _():
                arrive(number)

        block = block_of(step)
        pl.when(step > 0)(forward(step, block).wait_recv)
        row0 = pl.multiple_of(block * TILE, TILE)
        q = qkvbuf[0, pl.ds(row0, TILE), :]
        k = qkvbuf[1]
        v = qkvbuf[2]
        d = dbuf[block]
        cot = nt(d, w_ref[...]).astype(jnp.bfloat16)
        scores = nt(q, k) * inv_root + bias[pl.ds(block, 1), :]
        top = jnp.max(scores, axis=-1, keepdims=True)
        expo = jnp.exp(scores - top)
        probs = expo * (1.0 / jnp.sum(expo, axis=-1, keepdims=True))
        probs_b = probs.astype(jnp.bfloat16)
        att = nn(probs_b, v).astype(jnp.bfloat16)
        delta = jnp.sum(
            cot.astype(jnp.float32) * att.astype(jnp.float32), axis=-1, keepdims=True
        )
        dscores = (probs * (nt(cot, v) - delta)).astype(jnp.bfloat16)
        dqbuf[pl.ds(row0, TILE), :] = (nn(dscores, k) * inv_root).astype(jnp.bfloat16)

        hop = lax.rem(pick(step, [o[0] for o in ORDER]) + SIDE, SIDE)
        pl.when((step > 0) | away)(dq_copy(step, block, hop * 4 + slot_of_job).start)

        dkt[...] += tn(q, dscores)
        dvt[...] += tn(cot, probs_b)
        gw_ref[...] += tn(att, d)
        return carry

    lax.fori_loop(0, BLOCKS, body, 0)

    gw_copy = pltpu.make_async_remote_copy(
        src_ref=gwout, dst_ref=gwin, send_sem=x_send.at[1], recv_sem=x_recv.at[1],
        device_id=swap, device_id_type=MESH,
    )

    @pl.when(away)
    def _():
        gwout[...] = gw_ref[...].astype(jnp.bfloat16)
        gw_copy.start()

    kvbuf[0] = (dkt[...].T * inv_root).astype(jnp.bfloat16)
    kvbuf[1] = dvt[...].T.astype(jnp.bfloat16)

    def kv_copy(dz, target, recv):
        block = wrap(z, dz) * SIDE + target
        return pltpu.make_async_remote_copy(
            src_ref=kvbuf.at[:, pl.ds(pl.multiple_of(block * TILE, TILE), TILE)],
            dst_ref=grads_ref.at[pl.ds(1, 2), head],
            send_sem=kv_send.at[dz * 4 + target],
            recv_sem=kv_recv.at[recv],
            device_id={"dp": x * 2 + side, "seq": block},
            device_id_type=MESH,
        )

    def kv_mine(dz, target):
        return (y == target) & home if dz == 0 else None

    kv_keys = [(dz, target) for dz in (2, 1, 3, 0) for target in range(SIDE)]
    for key in kv_keys:
        unless(kv_mine(*key), kv_copy(*key, key[0] * 4 + slot_of_job).start)
    own_kv = pltpu.make_async_copy(
        kvbuf.at[:, pl.ds(pl.multiple_of(me * TILE, TILE), TILE)],
        grads_ref.at[pl.ds(1, 2), me],
        local_sem.at[5],
    )
    own_dq = pltpu.make_async_copy(
        dqbuf.at[pl.ds(pl.multiple_of(me * TILE, TILE), TILE)], grads_ref.at[0, me], local_sem.at[6]
    )

    @pl.when(home)
    def _():
        own_kv.start()
        own_dq.start()

    @pl.when(away)
    def _():
        gw_copy.wait_recv()
        gw_ref[...] = gwin[...].astype(jnp.float32)

    def moment(index, total):
        at = pl.ds(pl.multiple_of(index * rows, rows), rows)
        value = 0.9 * mom_ref[at, :] + 0.1 * gw_ref[at, :]
        mom_ref[at, :] = value
        return total + jnp.abs(value)

    total = lax.fori_loop(0, WORKERS, moment, jnp.zeros((rows, width), jnp.float32))
    scale = jnp.sum(total, axis=(0, 1), keepdims=True) / (rows * WORKERS * width) + 1e-06
    unscale = 1.0 / scale

    def compress(index, carry):
        at = pl.ds(pl.multiple_of(index * rows, rows), rows)
        value = mom_ref[at, :]
        code = (scale * jnp.tanh(value * unscale)).astype(jnp.bfloat16)
        sentbuf[at, :] = code
        werrbuf[at, :] = value - code.astype(jnp.float32)
        return carry

    lax.fori_loop(0, WORKERS, compress, 0)
    m_copies = []
    for index, peer in enumerate(workers):
        copy = pltpu.make_async_remote_copy(
            src_ref=sentbuf.at[pl.ds(pl.multiple_of(peer * rows, rows), rows)],
            dst_ref=landed.at[worker],
            send_sem=m_send.at[index],
            recv_sem=m_recv.at[index],
            device_id={"dp": peer},
            device_id_type=MESH,
        )
        copy.start()
        m_copies.append(copy)
    landed[worker] = sentbuf[pl.ds(pl.multiple_of(worker * rows, rows), rows), :]
    werr_out = pltpu.make_async_copy(werrbuf, werr_ref, local_sem.at[4])
    werr_out.start()

    for copy in m_copies:
        copy.wait_recv()
    average = landed[0].astype(jnp.float32)
    for index in range(1, WORKERS):
        average = average + landed[index].astype(jnp.float32)
    average = average / WORKERS
    server = jnp.sum(jnp.abs(average), axis=(0, 1), keepdims=True) / (rows * width) + 1e-06
    code = (server * jnp.tanh(average * (1.0 / server))).astype(jnp.bfloat16)
    syncbuf[...] = code
    serrbuf[...] = average - code.astype(jnp.float32)
    mine = sync_ref.at[pl.ds(pl.multiple_of(worker * rows, rows), rows)]
    s_copies = []
    for index, peer in enumerate(workers):
        copy = pltpu.make_async_remote_copy(
            src_ref=syncbuf,
            dst_ref=mine,
            send_sem=s_send.at[index],
            recv_sem=s_recv.at[index],
            device_id={"dp": peer},
            device_id_type=MESH,
        )
        copy.start()
        s_copies.append(copy)
    own_s = pltpu.make_async_copy(syncbuf, mine, local_sem.at[7])
    own_s.start()
    serr_out = pltpu.make_async_copy(serrbuf, serr_ref, local_sem.at[8])
    serr_out.start()

    for key in q_keys:
        unless(q_mine(*key), q_copy(*key, 0).wait_send)
    for copy in gather.every() + starts + m_copies:
        copy.wait_send()
    for copy in s_copies:
        copy.wait()

    @pl.when(away)
    def _():
        w_copy.wait_send()
        gw_copy.wait_send()

    for step in range(1, BLOCKS):
        forward(step, me).wait_send()

    for step in range(BLOCKS):
        unless(home if step == 0 else None, dq_copy(step, me, 0).wait_send)
    for key in kv_keys:
        unless(kv_mine(*key), kv_copy(*key, 0).wait_send)
    for slot in range(BLOCKS):
        mine = home & (slot_of_job == slot) if slot < 4 else None
        unless(mine, dq_copy(0, me, slot).wait_recv)
        unless(mine, kv_copy(0, 0, slot).wait_recv)

    @pl.when(home)
    def _():
        own_kv.wait()
        own_dq.wait()

    for copy in (own_s, werr_out, serr_out):
        copy.wait()


def body(qkv, tile_mask, d_out, w_out, momentum):
    tokens, head_size = qkv.shape[2], qkv.shape[4]
    width = d_out.shape[2]
    length = tokens * BLOCKS
    inv_root = 1.0 / math.sqrt(head_size)
    rows = head_size // WORKERS
    qkv_t = jnp.transpose(qkv[:, 0], (0, 2, 1, 3))
    vmem = pl.BlockSpec(memory_space=pltpu.VMEM)
    hbm = pl.BlockSpec(memory_space=pl.ANY)
    dma = pltpu.SemaphoreType.DMA
    grads, synced, worker_error, server_error = pl.pallas_call(
        functools.partial(kernel, inv_root),
        out_shape=(
            jax.ShapeDtypeStruct((3, HEADS, tokens, head_size), jnp.bfloat16),
            jax.ShapeDtypeStruct((head_size, width), jnp.bfloat16),
            jax.ShapeDtypeStruct((head_size, width), jnp.float32),
            jax.ShapeDtypeStruct((rows, width), jnp.float32),
        ),
        in_specs=[hbm, hbm, hbm, vmem, hbm],
        out_specs=(hbm, hbm, hbm, hbm),
        scratch_shapes=[
            pltpu.VMEM((3, length, head_size), jnp.bfloat16),
            pltpu.VMEM((BLOCKS, tokens, width), jnp.bfloat16),
            pltpu.VMEM((head_size, width), jnp.bfloat16),
            pltpu.VMEM((head_size, width), jnp.float32),
            pltpu.VMEM((BLOCKS, length), jnp.float32),
            pltpu.VMEM((length, head_size), jnp.bfloat16),
            pltpu.VMEM((head_size, length), jnp.float32),
            pltpu.VMEM((head_size, length), jnp.float32),
            pltpu.VMEM((2, length, head_size), jnp.bfloat16),
            pltpu.VMEM((head_size, width), jnp.float32),
            pltpu.VMEM((head_size, width), jnp.bfloat16),
            pltpu.VMEM((head_size, width), jnp.float32),
            pltpu.VMEM((WORKERS, rows, width), jnp.bfloat16),
            pltpu.VMEM((rows, width), jnp.bfloat16),
            pltpu.VMEM((rows, width), jnp.float32),
            pltpu.VMEM((head_size, width), jnp.bfloat16),
            pltpu.VMEM((head_size, width), jnp.bfloat16),
            dma((BLOCKS,)), dma((BLOCKS,)),
            dma((34,)), dma((34,)),
            dma((BLOCKS,)), dma((BLOCKS,)),
            dma((2,)), dma((3,)),
            dma((BLOCKS,)), dma((BLOCKS,)),
            dma((BLOCKS,)), dma((BLOCKS,)),
            dma((2,)), dma((2,)),
            dma((WORKERS - 1,)), dma((WORKERS - 1,)),
            dma((WORKERS - 1,)), dma((WORKERS - 1,)),
            dma((9,)),
        ],
        compiler_params=pltpu.CompilerParams(
            collective_id=0, has_side_effects=True, vmem_limit_bytes=56 << 20
        ),
    )(qkv_t, d_out[0], w_out[0], tile_mask, momentum[0])
    grad_qkv = jnp.transpose(grads, (0, 2, 1, 3))[:, None]
    return (grad_qkv, synced[None], worker_error[None, None], server_error[None])


def solution(mesh):
    placed = (
        P(None, "dp", "seq", None, None),
        P(),
        P("dp", "seq", None),
        P("seq", None, None),
        P("seq", None, None),
    )
    return jax.shard_map(
        body,
        mesh=mesh,
        in_specs=placed,
        out_specs=(
            P(None, "dp", "seq", None, None),
            P("seq", None, None),
            P("dp", "seq", None, None),
            P("seq", "dp", None),
        ),
        check_vma=False,
    )
```

time: 134 us -> 137 us (1.022)
  Pallas kernels: 123 us -> 126 us
    pallas_call x1, Pallas kernels: 123 us -> 126 us  [body(): pl.pallas_call(functools.partial(kernel, inv_root), out_shape=(jax.ShapeD...]
where the time goes in v3:
time: 137 us
  Pallas kernels  126 us (92%)
  local copies, waits for them, and re-layouts  10.1 us (7%)
    pallas_call x1, Pallas kernels, body(): pl.pallas_call(functools.partial(kernel, inv_root), out_shape=(jax.ShapeD...  126 us
    unnamed x11, local copies, waits for them, and re-layouts  10.1 us

profile of v3, /device:TPU:1, one launch (start us, length us, event | category | flops | bytes accessed | tf_op | source)
XLA Modules:
  0.0 136.7 jit_solution(2861203160575777580)
XLA Ops:
  0.6 3.0 %copy.12 = bf16[3,1,128,16,128]{4,2,3,0,1:T(8,128)(2,1)} copy(bf16[3,1,128,16,128]{4,3,2,1,0:T(8,128)(2,1)} %param.5) | data formatting | bytes 3145728 | tf_op args[0]
  3.6 125.9 %shard_map.84 = (bf16[3,16,128,128]{3,2,1,0:T(8,128)(2,1)}, bf16[128,3072]{1,0:T(8,128)(2,1)}, f32[128,3072]{1,0:T(8,128)}, f32[16,3072]{1,0:T(8,128)}) custom-call(bf16[3,16,128,128]{3,2,1,0:T(8,128)(2,1)} %bitcast.14, bf16[128,3072]{1,0:T(8,128)(2,1)} %bitcast.18, bf16[128,3072]{1,0:T(8,128)(2,1)} %bitcast.19, s32[8,16,16]{2,1,0:T(8,128)} %mask_ref.1, ...), custom_call_target="tpu_custom_call" | custom-call | tf_op jit(solution)/shard_map/pallas_call | solution.py:531
  129.5 0.0 copy-start.1
  129.5 3.6 %copy.10 = bf16[3,1,128,16,128]{4,3,2,1,0:T(8,128)(2,1)} copy(bf16[3,1,128,16,128]{4,2,3,0,1:T(8,128)(2,1)} %bitcast.16) | data formatting | bytes 3145728
  133.2 0.0 copy-start
  133.2 0.0 copy-done.1
  133.2 0.9 copy.16
  134.0 0.8 copy-done
  134.8 0.0 copy-start.2
  134.8 1.1 copy.17
  136.0 0.0 copy-done.2
  136.0 0.7 copy.18
Async XLA Ops:
  129.5 3.7 %copy-start.1 = (bf16[128,3072]{1,0:T(8,128)(2,1)S(1)}, bf16[128,3072]{1,0:T(8,128)(2,1)}, u32[]{:S(2)}) copy-start(bf16[128,3072]{1,0:T(8,128)(2,1)} %get-tuple-element.9) | copy-start | bytes 2359300
  133.2 1.7 %copy-start = (f32[128,3072]{1,0:T(8,128)S(1)}, f32[128,3072]{1,0:T(8,128)}, u32[]{:S(2)}) copy-start(f32[128,3072]{1,0:T(8,128)} %get-tuple-element.10) | copy-start | bytes 4718596
  134.8 1.1 copy-start.2

commit v4 on v3

--- a/solution.py
+++ b/solution.py
@@ -105,10 +105,10 @@
     qkv_ref, dout_ref, w_hbm, mask_ref, mom_hbm,
     grads_ref, sync_ref, werr_ref, serr_ref,
     qkvbuf, dbuf, w_ref, mom_ref, bias, dqbuf, dkt, dvt, kvbuf, gw_ref,
-    sentbuf, werrbuf, landed, syncbuf, serrbuf, gwout, gwin,
+    sentbuf, werrbuf, landed, parts, sums, syncbuf, serrbuf, gwout, gwin, jobmom,
     q_send, q_recv, d_send, d_recv, f_send, f_recv, i_send, i_recv,
     g_send, g_recv, kv_send, kv_recv, x_send, x_recv,
-    m_send, m_recv, s_send, s_recv, local_sem,
+    m_send, m_recv, p_send, p_recv, s_send, s_recv, local_sem,
 ):
     me = lax.axis_index("seq")
     z = me // SIDE
@@ -135,14 +135,16 @@
     )
     own_w = pltpu.make_async_copy(w_hbm, w_ref, local_sem.at[2])
     own_m = pltpu.make_async_copy(mom_hbm, mom_ref, local_sem.at[3])
+    home_m = pltpu.make_async_copy(mom_hbm, jobmom, local_sem.at[3])
 
     @pl.when(home)
     def _():
         own_d.start()
         own_q.start()
         own_w.start()
-
-    own_m.start()
+        home_m.start()
+
+    pl.when(away)(own_m.start)
 
     workers = [
         wrap(x, dx) * 2 + lax.rem(core + dc, 2)
@@ -275,7 +277,8 @@
         gather.bz(column + 2, 0).start()
         gather.bz(column + 2, 1).start()
 
-    own_m.wait()
+    pl.when(home)(home_m.wait)
+    pl.when(away)(own_m.wait)
     pl.when(away)(landing(1 - core).wait_recv)
     pl.when(home)(own_q.wait)
     pl.when(home)(own_w.wait)
@@ -284,6 +287,12 @@
         for source in range(SIDE):
             unless((y == source) & home if dz == 0 else None,
                    q_copy(dz, 0, 0, dz * 4 + source).wait_recv)
+
+    mom_copy = pltpu.make_async_remote_copy(
+        src_ref=mom_hbm, dst_ref=jobmom, send_sem=x_send.at[2], recv_sem=x_recv.at[2],
+        device_id=swap, device_id_type=MESH,
+    )
+    pl.when(away)(mom_copy.start)
 
     def arrive(step):
         if step == 2:
@@ -337,21 +346,30 @@
             device_id_type=MESH,
         )
 
-    def body(step, carry):
+    def load(ref, blocks):
+        return jnp.concatenate(
+            [ref[pl.ds(pl.multiple_of(b * TILE, TILE), TILE), :] for b in blocks], axis=0
+        )
+
+    def body(turn, carry):
         for number in (2, 4, 8, 10, 12, 14):
-            @pl.when(step == number)
+            @pl.when(turn * 2 == number)
             def _():
                 arrive(number)
 
-        block = block_of(step)
-        pl.when(step > 0)(forward(step, block).wait_recv)
-        row0 = pl.multiple_of(block * TILE, TILE)
-        q = qkvbuf[0, pl.ds(row0, TILE), :]
+        steps = (turn * 2, turn * 2 + 1)
+        blocks = [block_of(step) for step in steps]
+        pl.when(turn > 0)(forward(steps[0], blocks[0]).wait_recv)
+        forward(steps[1], blocks[1]).wait_recv()
+        q = load(qkvbuf.at[0], blocks)
         k = qkvbuf[1]
         v = qkvbuf[2]
-        d = dbuf[block]
+        d = jnp.concatenate([dbuf[b] for b in blocks], axis=0)
         cot = nt(d, w_ref[...]).astype(jnp.bfloat16)
-        scores = nt(q, k) * inv_root + bias[pl.ds(block, 1), :]
+        hidden = jnp.concatenate(
+            [jnp.broadcast_to(bias[pl.ds(b, 1), :], (TILE, bias.shape[1])) for b in blocks], axis=0
+        )
+        scores = nt(q, k) * inv_root + hidden
         top = jnp.max(scores, axis=-1, keepdims=True)
         expo = jnp.exp(scores - top)
         probs = expo * (1.0 / jnp.sum(expo, axis=-1, keepdims=True))
@@ -361,27 +379,80 @@
             cot.astype(jnp.float32) * att.astype(jnp.float32), axis=-1, keepdims=True
         )
         dscores = (probs * (nt(cot, v) - delta)).astype(jnp.bfloat16)
-        dqbuf[pl.ds(row0, TILE), :] = (nn(dscores, k) * inv_root).astype(jnp.bfloat16)
-
-        hop = lax.rem(pick(step, [o[0] for o in ORDER]) + SIDE, SIDE)
-        pl.when((step > 0) | away)(dq_copy(step, block, hop * 4 + slot_of_job).start)
+        dq = (nn(dscores, k) * inv_root).astype(jnp.bfloat16)
+        for index, block in enumerate(blocks):
+            dqbuf[pl.ds(pl.multiple_of(block * TILE, TILE), TILE), :] = (
+                dq[index * TILE:(index + 1) * TILE]
+            )
+        for step, block in zip(steps, blocks):
+            hop = lax.rem(pick(step, [o[0] for o in ORDER]) + SIDE, SIDE)
+            pl.when((step > 0) | away)(dq_copy(step, block, hop * 4 + slot_of_job).start)
 
         dkt[...] += tn(q, dscores)
         dvt[...] += tn(cot, probs_b)
         gw_ref[...] += tn(att, d)
         return carry
 
-    lax.fori_loop(0, BLOCKS, body, 0)
+    lax.fori_loop(0, BLOCKS // 2, body, 0)
 
     gw_copy = pltpu.make_async_remote_copy(
         src_ref=gwout, dst_ref=gwin, send_sem=x_send.at[1], recv_sem=x_recv.at[1],
         device_id=swap, device_id_type=MESH,
     )
 
+    def rows_at(index):
+        return pl.ds(pl.multiple_of(index * rows, rows), rows)
+
+    def compress_all(mom, grad, sent):
+        def moment(index, total):
+            at = rows_at(index)
+            value = 0.9 * mom[at, :] + 0.1 * grad[at, :].astype(jnp.float32)
+            mom[at, :] = value
+            return total + jnp.abs(value)
+
+        total = lax.fori_loop(0, WORKERS, moment, jnp.zeros((rows, width), jnp.float32))
+        scale = jnp.sum(total, axis=(0, 1), keepdims=True) / (rows * WORKERS * width) + 1e-06
+        unscale = 1.0 / scale
+
+        def compress(index, carry):
+            at = rows_at(index)
+            value = mom[at, :]
+            code = (scale * jnp.tanh(value * unscale)).astype(jnp.bfloat16)
+            if sent is not None:
+                sent[at, :] = code
+            werrbuf[at, :] = value - code.astype(jnp.float32)
+            return carry
+
+        lax.fori_loop(0, WORKERS, compress, 0)
+
+    gwout[...] = gw_ref[...].astype(jnp.bfloat16)
+
     @pl.when(away)
     def _():
-        gwout[...] = gw_ref[...].astype(jnp.bfloat16)
-        gw_copy.start()
+        mom_copy.wait_recv()
+
+    compress_all(jobmom, gwout, sentbuf)
+
+    turns = (2, 1, 3)
+
+    def pair(index):
+        return pl.ds(pl.multiple_of(index * 2 * rows, 2 * rows), 2 * rows)
+
+    m_copies = []
+    for index, dx in enumerate(turns):
+        copy = pltpu.make_async_remote_copy(
+            src_ref=sentbuf.at[pair(wrap(x, dx))],
+            dst_ref=landed.at[x],
+            send_sem=m_send.at[index],
+            recv_sem=m_recv.at[index],
+            device_id={"dp": wrap(x, dx) * 2 + core},
+            device_id_type=MESH,
+        )
+        copy.start()
+        m_copies.append(copy)
+    landed[x] = sentbuf[pair(x), :]
+    werr_out = pltpu.make_async_copy(werrbuf, werr_ref, local_sem.at[4])
+    pl.when(home)(werr_out.start)
 
     kvbuf[0] = (dkt[...].T * inv_root).astype(jnp.bfloat16)
     kvbuf[1] = dvt[...].T.astype(jnp.bfloat16)
@@ -417,84 +488,89 @@
         own_kv.start()
         own_dq.start()
 
-    @pl.when(away)
-    def _():
-        gw_copy.wait_recv()
-        gw_ref[...] = gwin[...].astype(jnp.float32)
-
-    def moment(index, total):
-        at = pl.ds(pl.multiple_of(index * rows, rows), rows)
-        value = 0.9 * mom_ref[at, :] + 0.1 * gw_ref[at, :]
-        mom_ref[at, :] = value
-        return total + jnp.abs(value)
-
-    total = lax.fori_loop(0, WORKERS, moment, jnp.zeros((rows, width), jnp.float32))
-    scale = jnp.sum(total, axis=(0, 1), keepdims=True) / (rows * WORKERS * width) + 1e-06
-    unscale = 1.0 / scale
-
-    def compress(index, carry):
-        at = pl.ds(pl.multiple_of(index * rows, rows), rows)
-        value = mom_ref[at, :]
-        code = (scale * jnp.tanh(value * unscale)).astype(jnp.bfloat16)
-        sentbuf[at, :] = code
-        werrbuf[at, :] = value - code.astype(jnp.float32)
-        return carry
-
-    lax.fori_loop(0, WORKERS, compress, 0)
-    m_copies = []
-    for index, peer in enumerate(workers):
-        copy = pltpu.make_async_remote_copy(
-            src_ref=sentbuf.at[pl.ds(pl.multiple_of(peer * rows, rows), rows)],
-            dst_ref=landed.at[worker],
-            send_sem=m_send.at[index],
-            recv_sem=m_recv.at[index],
-            device_id={"dp": peer},
-            device_id_type=MESH,
-        )
-        copy.start()
-        m_copies.append(copy)
-    landed[worker] = sentbuf[pl.ds(pl.multiple_of(worker * rows, rows), rows), :]
-    werr_out = pltpu.make_async_copy(werrbuf, werr_ref, local_sem.at[4])
-    werr_out.start()
-
     for copy in m_copies:
         copy.wait_recv()
-    average = landed[0].astype(jnp.float32)
-    for index in range(1, WORKERS):
-        average = average + landed[index].astype(jnp.float32)
-    average = average / WORKERS
+    partial = landed[0].astype(jnp.float32)
+    for index in range(1, SIDE):
+        partial = partial + landed[index].astype(jnp.float32)
+    partial = partial.astype(jnp.bfloat16)
+    parts[0] = partial[:rows]
+    parts[1] = partial[rows:]
+
+    def part_copy(c, recv, seq):
+        return pltpu.make_async_remote_copy(
+            src_ref=parts.at[c],
+            dst_ref=sums.at[recv],
+            send_sem=p_send.at[c],
+            recv_sem=p_recv.at[recv],
+            device_id={"dp": x * 2 + c, "seq": seq},
+            device_id_type=MESH,
+        )
+
+    @pl.when(home)
+    def _():
+        part_copy(1 - core, 0, me).start()
+        sums[0] = parts[core]
+
+    @pl.when(away)
+    def _():
+        part_copy(0, 1, partner).start()
+        part_copy(1, 1, partner).start()
+        gw_copy.start()
+        part_copy(0, 0, me).wait_recv()
+
+    part_copy(0, 1, partner).wait_recv()
+
+    average = (sums[0].astype(jnp.float32) + sums[1].astype(jnp.float32)) / WORKERS
     server = jnp.sum(jnp.abs(average), axis=(0, 1), keepdims=True) / (rows * width) + 1e-06
     code = (server * jnp.tanh(average * (1.0 / server))).astype(jnp.bfloat16)
-    syncbuf[...] = code
+    syncbuf[rows_at(worker), :] = code
     serrbuf[...] = average - code.astype(jnp.float32)
-    mine = sync_ref.at[pl.ds(pl.multiple_of(worker * rows, rows), rows)]
-    s_copies = []
-    for index, peer in enumerate(workers):
-        copy = pltpu.make_async_remote_copy(
-            src_ref=syncbuf,
-            dst_ref=mine,
-            send_sem=s_send.at[index],
-            recv_sem=s_recv.at[index],
-            device_id={"dp": peer},
-            device_id_type=MESH,
-        )
-        copy.start()
-        s_copies.append(copy)
-    own_s = pltpu.make_async_copy(syncbuf, mine, local_sem.at[7])
-    own_s.start()
+
+    def sync_copy(slot, index, dp):
+        at = syncbuf.at[rows_at(index)]
+        return pltpu.make_async_remote_copy(
+            src_ref=at, dst_ref=at, send_sem=s_send.at[slot], recv_sem=s_recv.at[slot],
+            device_id={"dp": dp}, device_id_type=MESH,
+        )
+
+    for slot, dx in enumerate(turns):
+        sync_copy(slot, worker, wrap(x, dx) * 2 + core).start()
+    sync_copy(3, worker, other).start()
     serr_out = pltpu.make_async_copy(serrbuf, serr_ref, local_sem.at[8])
     serr_out.start()
+
+    @pl.when(away)
+    def _():
+        gw_copy.wait_recv()
+        compress_all(mom_ref, gwin, None)
+        werr_out.start()
+
+    for slot, dx in enumerate(turns):
+        sync_copy(slot, worker, other).wait_recv()
+        sync_copy(4 + slot, wrap(x, -dx) * 2 + core, other).start()
+    for slot in range(3, 7):
+        sync_copy(slot, worker, other).wait_recv()
+    own_s = pltpu.make_async_copy(syncbuf, sync_ref, local_sem.at[7])
+    own_s.start()
 
     for key in q_keys:
         unless(q_mine(*key), q_copy(*key, 0).wait_send)
     for copy in gather.every() + starts + m_copies:
         copy.wait_send()
-    for copy in s_copies:
-        copy.wait()
+    for slot in range(7):
+        sync_copy(slot, worker, other).wait_send()
+
+    @pl.when(home)
+    def _():
+        part_copy(1 - core, 0, me).wait_send()
 
     @pl.when(away)
     def _():
+        part_copy(0, 1, partner).wait_send()
+        part_copy(1, 1, partner).wait_send()
         w_copy.wait_send()
+        mom_copy.wait_send()
         gw_copy.wait_send()
 
     for step in range(1, BLOCKS):
@@ -551,19 +627,23 @@
             pltpu.VMEM((head_size, width), jnp.float32),
             pltpu.VMEM((head_size, width), jnp.bfloat16),
             pltpu.VMEM((head_size, width), jnp.float32),
-            pltpu.VMEM((WORKERS, rows, width), jnp.bfloat16),
-            pltpu.VMEM((rows, width), jnp.bfloat16),
+            pltpu.VMEM((SIDE, 2 * rows, width), jnp.bfloat16),
+            pltpu.VMEM((2, rows, width), jnp.bfloat16),
+            pltpu.VMEM((2, rows, width), jnp.bfloat16),
+            pltpu.VMEM((head_size, width), jnp.bfloat16),
             pltpu.VMEM((rows, width), jnp.float32),
             pltpu.VMEM((head_size, width), jnp.bfloat16),
             pltpu.VMEM((head_size, width), jnp.bfloat16),
+            pltpu.VMEM((head_size, width), jnp.float32),
             dma((BLOCKS,)), dma((BLOCKS,)),
             dma((34,)), dma((34,)),
             dma((BLOCKS,)), dma((BLOCKS,)),
             dma((2,)), dma((3,)),
             dma((BLOCKS,)), dma((BLOCKS,)),
             dma((BLOCKS,)), dma((BLOCKS,)),
+            dma((3,)), dma((3,)),
+            dma((SIDE - 1,)), dma((SIDE - 1,)),
             dma((2,)), dma((2,)),
-            dma((WORKERS - 1,)), dma((WORKERS - 1,)),
             dma((WORKERS - 1,)), dma((WORKERS - 1,)),
             dma((9,)),
         ],

time: 137 us -> 124 us (0.905)
  Pallas kernels: 126 us -> 113 us
    pallas_call x1, Pallas kernels: 126 us -> 113 us  [body(): pl.pallas_call(functools.partial(kernel, inv_root), out_shape=(jax.ShapeD...]
where the time goes in v4:
time: 124 us; the launch traced here: 123 us
  Pallas kernels  113 us (91%)
  local copies, waits for them, and re-layouts  10.1 us (8%)
    pallas_call x1, Pallas kernels, body(): pl.pallas_call(functools.partial(kernel, inv_root), out_shape=(jax.ShapeD...  113 us
    unnamed x11, local copies, waits for them, and re-layouts  10.1 us

profile of v4, /device:TPU:1, one launch (start us, length us, event | category | flops | bytes accessed | tf_op | source)
XLA Modules:
  0.0 123.3 jit_solution(13750517353119172305)
XLA Ops:
  0.6 3.0 %copy.12 = bf16[3,1,128,16,128]{4,2,3,0,1:T(8,128)(2,1)} copy(bf16[3,1,128,16,128]{4,3,2,1,0:T(8,128)(2,1)} %param.5) | data formatting | bytes 3145728 | tf_op args[0]
  3.6 112.6 %shard_map.84 = (bf16[3,16,128,128]{3,2,1,0:T(8,128)(2,1)}, bf16[128,3072]{1,0:T(8,128)(2,1)}, f32[128,3072]{1,0:T(8,128)}, f32[16,3072]{1,0:T(8,128)}) custom-call(bf16[3,16,128,128]{3,2,1,0:T(8,128)(2,1)} %bitcast.14, bf16[128,3072]{1,0:T(8,128)(2,1)} %bitcast.18, bf16[128,3072]{1,0:T(8,128)(2,1)} %bitcast.19, s32[8,16,16]{2,1,0:T(8,128)} %mask_ref.1, ...), custom_call_target="tpu_custom_call" | custom-call | tf_op jit(solution)/shard_map/pallas_call | solution.py:607
  116.2 0.0 copy-start.1
  116.2 3.6 %copy.10 = bf16[3,1,128,16,128]{4,3,2,1,0:T(8,128)(2,1)} copy(bf16[3,1,128,16,128]{4,2,3,0,1:T(8,128)(2,1)} %bitcast.16) | data formatting | bytes 3145728
  119.8 0.0 copy-start
  119.8 0.0 copy-done.1
  119.8 0.9 copy.16
  120.7 0.8 copy-done
  121.5 0.0 copy-start.2
  121.5 1.1 copy.17
  122.7 0.0 copy-done.2
  122.7 0.7 copy.18
Async XLA Ops:
  116.2 3.7 %copy-start.1 = (bf16[128,3072]{1,0:T(8,128)(2,1)S(1)}, bf16[128,3072]{1,0:T(8,128)(2,1)}, u32[]{:S(2)}) copy-start(bf16[128,3072]{1,0:T(8,128)(2,1)} %get-tuple-element.9) | copy-start | bytes 2359300
  119.8 1.7 %copy-start = (f32[128,3072]{1,0:T(8,128)S(1)}, f32[128,3072]{1,0:T(8,128)}, u32[]{:S(2)}) copy-start(f32[128,3072]{1,0:T(8,128)} %get-tuple-element.10) | copy-start | bytes 4718596
  121.5 1.1 copy-start.2

commit v5 on v4

--- a/solution.py
+++ b/solution.py
@@ -104,9 +104,9 @@
     inv_root,
     qkv_ref, dout_ref, w_hbm, mask_ref, mom_hbm,
     grads_ref, sync_ref, werr_ref, serr_ref,
-    qkvbuf, dbuf, w_ref, mom_ref, bias, dqbuf, dkt, dvt, kvbuf, gw_ref,
+    tokenwise, headwise, qkvbuf, dbuf, w_ref, mom_ref, bias, dqbuf, dkt, dvt, kvbuf, gw_ref,
     sentbuf, werrbuf, landed, parts, sums, syncbuf, serrbuf, gwout, gwin, jobmom,
-    q_send, q_recv, d_send, d_recv, f_send, f_recv, i_send, i_recv,
+    q_in, q_send, q_recv, d_send, d_recv, f_send, f_recv, i_send, i_recv,
     g_send, g_recv, kv_send, kv_recv, x_send, x_recv,
     m_send, m_recv, p_send, p_recv, s_send, s_recv, local_sem,
 ):
@@ -130,8 +130,11 @@
     slot_of_job = lax.rem(y, 2) * 2 + core
 
     own_d = pltpu.make_async_copy(dout_ref, dbuf.at[me], local_sem.at[0])
+    all_q = [pltpu.make_async_copy(qkv_ref.at[p], tokenwise.at[p], q_in.at[p]) for p in range(3)]
+    for copy in all_q:
+        copy.start()
     own_q = pltpu.make_async_copy(
-        qkv_ref.at[:, me], qkvbuf.at[:, pl.ds(me * TILE, TILE)], local_sem.at[1]
+        headwise.at[:, me], qkvbuf.at[:, pl.ds(me * TILE, TILE)], local_sem.at[1]
     )
     own_w = pltpu.make_async_copy(w_hbm, w_ref, local_sem.at[2])
     own_m = pltpu.make_async_copy(mom_hbm, mom_ref, local_sem.at[3])
@@ -140,7 +143,6 @@
     @pl.when(home)
     def _():
         own_d.start()
-        own_q.start()
         own_w.start()
         home_m.start()
 
@@ -201,7 +203,7 @@
         z2, y2 = wrap(z, dz), 2 * core + u
         theirs = z2 * SIDE + jnp.where(core == c, y2, 3 - y2)
         return pltpu.make_async_remote_copy(
-            src_ref=qkv_ref.at[:, theirs],
+            src_ref=headwise.at[:, theirs],
             dst_ref=qkvbuf.at[:, pl.ds(me * TILE, TILE)],
             send_sem=q_send.at[dz * 4 + u * 2 + c],
             recv_sem=q_recv.at[recv],
@@ -219,8 +221,12 @@
             pl.when(jnp.logical_not(mine))(action)
 
     q_keys = [(dz, u, c) for dz in range(SIDE) for u in range(2) for c in range(2)]
+    for p in range(3):
+        all_q[p].wait()
+        headwise[p] = jnp.swapaxes(tokenwise[p], 0, 1)
     for key in q_keys:
         unless(q_mine(*key), q_copy(*key, key[0] * 4 + y).start)
+    pl.when(home)(own_q.start)
 
     gather = Gather(dbuf, z, columns, core * HALF, d_send, d_recv)
 
@@ -425,35 +431,6 @@
 
         lax.fori_loop(0, WORKERS, compress, 0)
 
-    gwout[...] = gw_ref[...].astype(jnp.bfloat16)
-
-    @pl.when(away)
-    def _():
-        mom_copy.wait_recv()
-
-    compress_all(jobmom, gwout, sentbuf)
-
-    turns = (2, 1, 3)
-
-    def pair(index):
-        return pl.ds(pl.multiple_of(index * 2 * rows, 2 * rows), 2 * rows)
-
-    m_copies = []
-    for index, dx in enumerate(turns):
-        copy = pltpu.make_async_remote_copy(
-            src_ref=sentbuf.at[pair(wrap(x, dx))],
-            dst_ref=landed.at[x],
-            send_sem=m_send.at[index],
-            recv_sem=m_recv.at[index],
-            device_id={"dp": wrap(x, dx) * 2 + core},
-            device_id_type=MESH,
-        )
-        copy.start()
-        m_copies.append(copy)
-    landed[x] = sentbuf[pair(x), :]
-    werr_out = pltpu.make_async_copy(werrbuf, werr_ref, local_sem.at[4])
-    pl.when(home)(werr_out.start)
-
     kvbuf[0] = (dkt[...].T * inv_root).astype(jnp.bfloat16)
     kvbuf[1] = dvt[...].T.astype(jnp.bfloat16)
 
@@ -488,6 +465,35 @@
         own_kv.start()
         own_dq.start()
 
+    gwout[...] = gw_ref[...].astype(jnp.bfloat16)
+
+    @pl.when(away)
+    def _():
+        mom_copy.wait_recv()
+
+    compress_all(jobmom, gwout, sentbuf)
+
+    turns = (2, 1, 3)
+
+    def pair(index):
+        return pl.ds(pl.multiple_of(index * 2 * rows, 2 * rows), 2 * rows)
+
+    m_copies = []
+    for index, dx in enumerate(turns):
+        copy = pltpu.make_async_remote_copy(
+            src_ref=sentbuf.at[pair(wrap(x, dx))],
+            dst_ref=landed.at[x],
+            send_sem=m_send.at[index],
+            recv_sem=m_recv.at[index],
+            device_id={"dp": wrap(x, dx) * 2 + core},
+            device_id_type=MESH,
+        )
+        copy.start()
+        m_copies.append(copy)
+    landed[x] = sentbuf[pair(x), :]
+    werr_out = pltpu.make_async_copy(werrbuf, werr_ref, local_sem.at[4])
+    pl.when(home)(werr_out.start)
+
     for copy in m_copies:
         copy.wait_recv()
     partial = landed[0].astype(jnp.float32)
@@ -594,13 +600,34 @@
         copy.wait()
 
 
+def finish(
+    grads_in, sync_in, werr_in, serr_in, grads_out, sync_out, werr_out, serr_out,
+    before, after, sync, werr, serr, in_sem, out_sem,
+):
+    loads = [pltpu.make_async_copy(grads_in.at[p], before.at[p], in_sem.at[p]) for p in range(3)]
+    stores = [pltpu.make_async_copy(after.at[p], grads_out.at[p], out_sem.at[p]) for p in range(3)]
+    plain = ((werr_in, werr, werr_out), (sync_in, sync, sync_out), (serr_in, serr, serr_out))
+    for index, (source, buf, target) in enumerate(plain):
+        loads.append(pltpu.make_async_copy(source, buf, in_sem.at[3 + index]))
+        stores.append(pltpu.make_async_copy(buf, target, out_sem.at[3 + index]))
+    for load in loads:
+        load.start()
+    for p in range(3):
+        loads[p].wait()
+        after[p] = jnp.swapaxes(before[p], 0, 1)
+        stores[p].start()
+        loads[3 + p].wait()
+        stores[3 + p].start()
+    for store in stores:
+        store.wait()
+
+
 def body(qkv, tile_mask, d_out, w_out, momentum):
     tokens, head_size = qkv.shape[2], qkv.shape[4]
     width = d_out.shape[2]
     length = tokens * BLOCKS
     inv_root = 1.0 / math.sqrt(head_size)
     rows = head_size // WORKERS
-    qkv_t = jnp.transpose(qkv[:, 0], (0, 2, 1, 3))
     vmem = pl.BlockSpec(memory_space=pltpu.VMEM)
     hbm = pl.BlockSpec(memory_space=pl.ANY)
     dma = pltpu.SemaphoreType.DMA
@@ -615,6 +642,8 @@
         in_specs=[hbm, hbm, hbm, vmem, hbm],
         out_specs=(hbm, hbm, hbm, hbm),
         scratch_shapes=[
+            pltpu.VMEM((3, tokens, HEADS, head_size), jnp.bfloat16),
+            pltpu.VMEM((3, HEADS, tokens, head_size), jnp.bfloat16),
             pltpu.VMEM((3, length, head_size), jnp.bfloat16),
             pltpu.VMEM((BLOCKS, tokens, width), jnp.bfloat16),
             pltpu.VMEM((head_size, width), jnp.bfloat16),
@@ -635,7 +664,7 @@
             pltpu.VMEM((head_size, width), jnp.bfloat16),
             pltpu.VMEM((head_size, width), jnp.bfloat16),
             pltpu.VMEM((head_size, width), jnp.float32),
-            dma((BLOCKS,)), dma((BLOCKS,)),
+            dma((3,)), dma((BLOCKS,)), dma((BLOCKS,)),
             dma((34,)), dma((34,)),
             dma((BLOCKS,)), dma((BLOCKS,)),
             dma((2,)), dma((3,)),
@@ -650,8 +679,28 @@
         compiler_params=pltpu.CompilerParams(
             collective_id=0, has_side_effects=True, vmem_limit_bytes=56 << 20
         ),
-    )(qkv_t, d_out[0], w_out[0], tile_mask, momentum[0])
-    grad_qkv = jnp.transpose(grads, (0, 2, 1, 3))[:, None]
+    )(qkv[:, 0], d_out[0], w_out[0], tile_mask, momentum[0])
+    grad_qkv, synced, worker_error, server_error = pl.pallas_call(
+        finish,
+        out_shape=(
+            jax.ShapeDtypeStruct((3, tokens, HEADS, head_size), jnp.bfloat16),
+            jax.ShapeDtypeStruct((head_size, width), jnp.bfloat16),
+            jax.ShapeDtypeStruct((head_size, width), jnp.float32),
+            jax.ShapeDtypeStruct((rows, width), jnp.float32),
+        ),
+        in_specs=[hbm] * 4,
+        out_specs=(hbm,) * 4,
+        scratch_shapes=[
+            pltpu.VMEM((3, HEADS, tokens, head_size), jnp.bfloat16),
+            pltpu.VMEM((3, tokens, HEADS, head_size), jnp.bfloat16),
+            pltpu.VMEM((head_size, width), jnp.bfloat16),
+            pltpu.VMEM((head_size, width), jnp.float32),
+            pltpu.VMEM((rows, width), jnp.float32),
+            dma((6,)), dma((6,)),
+        ],
+        compiler_params=pltpu.CompilerParams(vmem_limit_bytes=56 << 20),
+    )(grads, synced, worker_error, server_error)
+    grad_qkv = grad_qkv[:, None]
     return (grad_qkv, synced[None], worker_error[None, None], server_error[None])
 
 

time: 124 us -> 117 us (0.944)
  local copies, waits for them, and re-layouts: 10.1 us -> 0 us
  Pallas kernels: 113 us -> 116 us
    unnamed x11 -> x0, local copies, waits for them, and re-layouts: 10.1 us -> none
    pallas_call x0 -> x1, Pallas kernels: none -> 3.8 us  [body(): pl.pallas_call(finish, out_shape=(jax.ShapeDtypeStruct((3, tokens, HEADS,...]
where the time goes in v5:
time: 117 us
  Pallas kernels  116 us (99%)
    pallas_call x1, Pallas kernels, body(): pl.pallas_call(functools.partial(kernel, inv_root), out_shape=(jax.ShapeD...  113 us
    pallas_call x1, Pallas kernels, body(): pl.pallas_call(finish, out_shape=(jax.ShapeDtypeStruct((3, tokens, HEADS,...  3.8 us

profile of v5, /device:TPU:1, one launch (start us, length us, event | category | flops | bytes accessed | tf_op | source)
XLA Modules:
  0.0 116.9 jit_solution(4521990402349502064)
XLA Ops:
  0.6 112.5 %shard_map.84 = (bf16[3,16,128,128]{3,2,1,0:T(8,128)(2,1)}, bf16[128,3072]{1,0:T(8,128)(2,1)}, f32[128,3072]{1,0:T(8,128)}, f32[16,3072]{1,0:T(8,128)}) custom-call(bf16[3,128,16,128]{3,2,1,0:T(8,128)(2,1)} %bitcast.10, bf16[128,3072]{1,0:T(8,128)(2,1)} %bitcast.12, bf16[128,3072]{1,0:T(8,128)(2,1)} %bitcast.13, s32[8,16,16]{2,1,0:T(8,128)} %mask_ref.1, ...), custom_call_target="tpu_custom_call" | custom-call | tf_op jit(solution)/shard_map/pallas_call | solution.py:634
  113.1 3.8 %shard_map.85 = (bf16[3,128,16,128]{3,2,1,0:T(8,128)(2,1)}, bf16[128,3072]{1,0:T(8,128)(2,1)}, f32[128,3072]{1,0:T(8,128)}, f32[16,3072]{1,0:T(8,128)}) custom-call(bf16[3,16,128,128]{3,2,1,0:T(8,128)(2,1)} %get-tuple-element.12.grads_in, bf16[128,3072]{1,0:T(8,128)(2,1)} %get-tuple-element.13.sync_in, f32[128,3072]{1,0:T(8,128)} %get-tuple-element.14.werr_in, ...), custom_call_target="tpu_custom_call" | custom-call | tf_op jit(solution)/shard_map/pallas_call | solution.py:683

commit v6 on v5

--- a/solution.py
+++ b/solution.py
@@ -104,7 +104,7 @@
     inv_root,
     qkv_ref, dout_ref, w_hbm, mask_ref, mom_hbm,
     grads_ref, sync_ref, werr_ref, serr_ref,
-    tokenwise, headwise, qkvbuf, dbuf, w_ref, mom_ref, bias, dqbuf, dkt, dvt, kvbuf, gw_ref,
+    gland, tokenwise, headwise, qkvbuf, dbuf, w_ref, mom_ref, bias, dqbuf, dkt, dvt, kvbuf, gw_ref,
     sentbuf, werrbuf, landed, parts, sums, syncbuf, serrbuf, gwout, gwin, jobmom,
     q_in, q_send, q_recv, d_send, d_recv, f_send, f_recv, i_send, i_recv,
     g_send, g_recv, kv_send, kv_recv, x_send, x_recv,
@@ -221,13 +221,6 @@
             pl.when(jnp.logical_not(mine))(action)
 
     q_keys = [(dz, u, c) for dz in range(SIDE) for u in range(2) for c in range(2)]
-    for p in range(3):
-        all_q[p].wait()
-        headwise[p] = jnp.swapaxes(tokenwise[p], 0, 1)
-    for key in q_keys:
-        unless(q_mine(*key), q_copy(*key, key[0] * 4 + y).start)
-    pl.when(home)(own_q.start)
-
     gather = Gather(dbuf, z, columns, core * HALF, d_send, d_recv)
 
     def launch(column):
@@ -255,9 +248,23 @@
     def pass_on(dz, column):
         forward(ORDER.index((dz, column)), gather.block(dz, column)).start()
 
-    pl.when(home)(own_d.wait)
-    pl.when(away)(landing(core).wait_recv)
-    launch(0)
+    @pl.when(home)
+    def _():
+        own_d.wait()
+        launch(0)
+
+    for p in range(3):
+        all_q[p].wait()
+        headwise[p] = jnp.swapaxes(tokenwise[p], 0, 1)
+    for key in q_keys:
+        unless(q_mine(*key), q_copy(*key, key[0] * 4 + y).start)
+    pl.when(home)(own_q.start)
+
+    @pl.when(away)
+    def _():
+        landing(core).wait_recv()
+        launch(0)
+
     landing(2).wait_recv()
     launch(1)
     pass_on(0, 1)
@@ -345,7 +352,7 @@
     def dq_copy(step, block, recv):
         return pltpu.make_async_remote_copy(
             src_ref=dqbuf.at[pl.ds(pl.multiple_of(block * TILE, TILE), TILE)],
-            dst_ref=grads_ref.at[0, head],
+            dst_ref=gland.at[0, head],
             send_sem=g_send.at[step],
             recv_sem=g_recv.at[recv],
             device_id={"dp": x * 2 + side, "seq": block},
@@ -359,7 +366,7 @@
 
     def body(turn, carry):
         for number in (2, 4, 8, 10, 12, 14):
-            @pl.when(turn * 2 == number)
+            @pl.when(turn * 2 + 2 == number)
             def _():
                 arrive(number)
 
@@ -431,14 +438,14 @@
 
         lax.fori_loop(0, WORKERS, compress, 0)
 
-    kvbuf[0] = (dkt[...].T * inv_root).astype(jnp.bfloat16)
-    kvbuf[1] = dvt[...].T.astype(jnp.bfloat16)
+    kvbuf[0] = (dkt[...] * inv_root).astype(jnp.bfloat16).T
+    kvbuf[1] = dvt[...].astype(jnp.bfloat16).T
 
     def kv_copy(dz, target, recv):
         block = wrap(z, dz) * SIDE + target
         return pltpu.make_async_remote_copy(
             src_ref=kvbuf.at[:, pl.ds(pl.multiple_of(block * TILE, TILE), TILE)],
-            dst_ref=grads_ref.at[pl.ds(1, 2), head],
+            dst_ref=gland.at[pl.ds(1, 2), head],
             send_sem=kv_send.at[dz * 4 + target],
             recv_sem=kv_recv.at[recv],
             device_id={"dp": x * 2 + side, "seq": block},
@@ -453,11 +460,11 @@
         unless(kv_mine(*key), kv_copy(*key, key[0] * 4 + slot_of_job).start)
     own_kv = pltpu.make_async_copy(
         kvbuf.at[:, pl.ds(pl.multiple_of(me * TILE, TILE), TILE)],
-        grads_ref.at[pl.ds(1, 2), me],
+        gland.at[pl.ds(1, 2), me],
         local_sem.at[5],
     )
     own_dq = pltpu.make_async_copy(
-        dqbuf.at[pl.ds(pl.multiple_of(me * TILE, TILE), TILE)], grads_ref.at[0, me], local_sem.at[6]
+        dqbuf.at[pl.ds(pl.multiple_of(me * TILE, TILE), TILE)], gland.at[0, me], local_sem.at[6]
     )
 
     @pl.when(home)
@@ -494,6 +501,16 @@
     werr_out = pltpu.make_async_copy(werrbuf, werr_ref, local_sem.at[4])
     pl.when(home)(werr_out.start)
 
+    g_out = [
+        pltpu.make_async_copy(tokenwise.at[p], grads_ref.at[p], q_in.at[p]) for p in range(3)
+    ]
+    pl.when(home)(own_dq.wait)
+    for slot in range(BLOCKS):
+        mine = home & (slot_of_job == slot) if slot < 4 else None
+        unless(mine, dq_copy(0, me, slot).wait_recv)
+    tokenwise[0] = jnp.swapaxes(gland[0], 0, 1)
+    g_out[0].start()
+
     for copy in m_copies:
         copy.wait_recv()
     partial = landed[0].astype(jnp.float32)
@@ -546,6 +563,14 @@
     serr_out = pltpu.make_async_copy(serrbuf, serr_ref, local_sem.at[8])
     serr_out.start()
 
+    pl.when(home)(own_kv.wait)
+    for slot in range(BLOCKS):
+        mine = home & (slot_of_job == slot) if slot < 4 else None
+        unless(mine, kv_copy(0, 0, slot).wait_recv)
+    for p in range(1, 3):
+        tokenwise[p] = jnp.swapaxes(gland[p], 0, 1)
+        g_out[p].start()
+
     @pl.when(away)
     def _():
         gw_copy.wait_recv()
@@ -586,38 +611,30 @@
         unless(home if step == 0 else None, dq_copy(step, me, 0).wait_send)
     for key in kv_keys:
         unless(kv_mine(*key), kv_copy(*key, 0).wait_send)
-    for slot in range(BLOCKS):
-        mine = home & (slot_of_job == slot) if slot < 4 else None
-        unless(mine, dq_copy(0, me, slot).wait_recv)
-        unless(mine, kv_copy(0, 0, slot).wait_recv)
-
-    @pl.when(home)
-    def _():
-        own_kv.wait()
-        own_dq.wait()
-
-    for copy in (own_s, werr_out, serr_out):
+    for copy in [own_s, werr_out, serr_out] + g_out:
         copy.wait()
 
 
 def finish(
     grads_in, sync_in, werr_in, serr_in, grads_out, sync_out, werr_out, serr_out,
-    before, after, sync, werr, serr, in_sem, out_sem,
+    grads, sync, werr, serr, in_sem, out_sem,
 ):
-    loads = [pltpu.make_async_copy(grads_in.at[p], before.at[p], in_sem.at[p]) for p in range(3)]
-    stores = [pltpu.make_async_copy(after.at[p], grads_out.at[p], out_sem.at[p]) for p in range(3)]
-    plain = ((werr_in, werr, werr_out), (sync_in, sync, sync_out), (serr_in, serr, serr_out))
-    for index, (source, buf, target) in enumerate(plain):
-        loads.append(pltpu.make_async_copy(source, buf, in_sem.at[3 + index]))
-        stores.append(pltpu.make_async_copy(buf, target, out_sem.at[3 + index]))
+    loads, stores = [], []
+    chunks = [(grads_in, grads, grads_out, p, 1) for p in range(3)]
+    rows = werr.shape[0] // 2
+    for half in range(2):
+        chunks.append((werr_in, werr, werr_out, half * rows, rows))
+    chunks.append((sync_in, sync, sync_out, 0, sync.shape[0]))
+    chunks.append((serr_in, serr, serr_out, 0, serr.shape[0]))
+    for index, (source, buf, target, first, count) in enumerate(chunks):
+        at = pl.ds(first, count)
+        loads.append(pltpu.make_async_copy(source.at[at], buf.at[at], in_sem.at[index]))
+        stores.append(pltpu.make_async_copy(buf.at[at], target.at[at], out_sem.at[index]))
     for load in loads:
         load.start()
-    for p in range(3):
-        loads[p].wait()
-        after[p] = jnp.swapaxes(before[p], 0, 1)
-        stores[p].start()
-        loads[3 + p].wait()
-        stores[3 + p].start()
+    for load, store in zip(loads, stores):
+        load.wait()
+        store.start()
     for store in stores:
         store.wait()
 
@@ -634,7 +651,7 @@
     grads, synced, worker_error, server_error = pl.pallas_call(
         functools.partial(kernel, inv_root),
         out_shape=(
-            jax.ShapeDtypeStruct((3, HEADS, tokens, head_size), jnp.bfloat16),
+            jax.ShapeDtypeStruct((3, tokens, HEADS, head_size), jnp.bfloat16),
             jax.ShapeDtypeStruct((head_size, width), jnp.bfloat16),
             jax.ShapeDtypeStruct((head_size, width), jnp.float32),
             jax.ShapeDtypeStruct((rows, width), jnp.float32),
@@ -642,6 +659,7 @@
         in_specs=[hbm, hbm, hbm, vmem, hbm],
         out_specs=(hbm, hbm, hbm, hbm),
         scratch_shapes=[
+            pltpu.VMEM((3, HEADS, tokens, head_size), jnp.bfloat16),
             pltpu.VMEM((3, tokens, HEADS, head_size), jnp.bfloat16),
             pltpu.VMEM((3, HEADS, tokens, head_size), jnp.bfloat16),
             pltpu.VMEM((3, length, head_size), jnp.bfloat16),
@@ -691,12 +709,11 @@
         in_specs=[hbm] * 4,
         out_specs=(hbm,) * 4,
         scratch_shapes=[
-            pltpu.VMEM((3, HEADS, tokens, head_size), jnp.bfloat16),
             pltpu.VMEM((3, tokens, HEADS, head_size), jnp.bfloat16),
             pltpu.VMEM((head_size, width), jnp.bfloat16),
             pltpu.VMEM((head_size, width), jnp.float32),
             pltpu.VMEM((rows, width), jnp.float32),
-            dma((6,)), dma((6,)),
+            dma((7,)), dma((7,)),
         ],
         compiler_params=pltpu.CompilerParams(vmem_limit_bytes=56 << 20),
     )(grads, synced, worker_error, server_error)

time: 117 us -> 112 us (0.957)
  Pallas kernels: 116 us -> 111 us
    pallas_call x1, Pallas kernels: 113 us -> 108 us  [body(): pl.pallas_call(functools.partial(kernel, inv_root), out_shape=(jax.ShapeD...]
where the time goes in v6:
time: 112 us
  Pallas kernels  111 us (99%)
    pallas_call x1, Pallas kernels, body(): pl.pallas_call(functools.partial(kernel, inv_root), out_shape=(jax.ShapeD...  108 us
    pallas_call x1, Pallas kernels, body(): pl.pallas_call(finish, out_shape=(jax.ShapeDtypeStruct((3, tokens, HEADS,...  3.45 us

profile of v6, /device:TPU:1, one launch (start us, length us, event | category | flops | bytes accessed | tf_op | source)
XLA Modules:
  0.0 111.8 jit_solution(1142771383597716767)
XLA Ops:
  0.6 107.7 %shard_map.84 = (bf16[3,128,16,128]{3,2,1,0:T(8,128)(2,1)}, bf16[128,3072]{1,0:T(8,128)(2,1)}, f32[128,3072]{1,0:T(8,128)}, f32[16,3072]{1,0:T(8,128)}) custom-call(bf16[3,128,16,128]{3,2,1,0:T(8,128)(2,1)} %bitcast.10, bf16[128,3072]{1,0:T(8,128)(2,1)} %bitcast.12, bf16[128,3072]{1,0:T(8,128)(2,1)} %bitcast.13, s32[8,16,16]{2,1,0:T(8,128)} %mask_ref.1, ...), custom_call_target="tpu_custom_call" | custom-call | tf_op jit(solution)/shard_map/pallas_call | solution.py:651
  108.4 3.5 %shard_map.85 = (bf16[3,128,16,128]{3,2,1,0:T(8,128)(2,1)}, bf16[128,3072]{1,0:T(8,128)(2,1)}, f32[128,3072]{1,0:T(8,128)}, f32[16,3072]{1,0:T(8,128)}) custom-call(bf16[3,128,16,128]{3,2,1,0:T(8,128)(2,1)} %get-tuple-element.12.grads_in, bf16[128,3072]{1,0:T(8,128)(2,1)} %get-tuple-element.13.sync_in, f32[128,3072]{1,0:T(8,128)} %get-tuple-element.14.werr_in, ...), custom_call_target="tpu_custom_call" | custom-call | tf_op jit(solution)/shard_map/pallas_call | solution.py:701

commit v7 on v6

--- a/solution.py
+++ b/solution.py
@@ -163,6 +163,9 @@
         )
     for peer in workers[:-1]:
         pl.semaphore_signal(barrier, inc=1, device_id={"dp": peer}, device_id_type=MESH)
+    for p in range(3):
+        all_q[p].wait()
+        headwise[p] = jnp.swapaxes(tokenwise[p], 0, 1)
     pl.semaphore_wait(barrier, len(plane) + len(workers) - 1)
 
     starts = []
@@ -197,7 +200,6 @@
         src_ref=w_hbm, dst_ref=w_ref, send_sem=x_send.at[0], recv_sem=x_recv.at[0],
         device_id=swap, device_id_type=MESH,
     )
-    pl.when(away)(w_copy.start)
 
     def q_copy(dz, u, c, recv):
         z2, y2 = wrap(z, dz), 2 * core + u
@@ -253,12 +255,15 @@
         own_d.wait()
         launch(0)
 
-    for p in range(3):
-        all_q[p].wait()
-        headwise[p] = jnp.swapaxes(tokenwise[p], 0, 1)
-    for key in q_keys:
-        unless(q_mine(*key), q_copy(*key, key[0] * 4 + y).start)
-    pl.when(home)(own_q.start)
+    def send_q():
+        for key in q_keys:
+            unless(q_mine(*key), q_copy(*key, key[0] * 4 + y).start)
+
+    @pl.when(home)
+    def _():
+        send_q()
+        own_q.start()
+
 
     @pl.when(away)
     def _():
@@ -268,6 +273,14 @@
     landing(2).wait_recv()
     launch(1)
     pass_on(0, 1)
+
+    @pl.when(away)
+    def _():
+        for copy in starts:
+            copy.wait_send()
+        w_copy.start()
+        send_q()
+
 
     tiles = mask_ref[head // (HEADS // GROUPS)]
     for j in range(BLOCKS):
@@ -438,6 +451,36 @@
 
         lax.fori_loop(0, WORKERS, compress, 0)
 
+    gw_copy = pltpu.make_async_remote_copy(
+        src_ref=gwout, dst_ref=gwin, send_sem=x_send.at[1], recv_sem=x_recv.at[1],
+        device_id=swap, device_id_type=MESH,
+    )
+
+    def rows_at(index):
+        return pl.ds(pl.multiple_of(index * rows, rows), rows)
+
+    def compress_all(mom, grad, sent):
+        def moment(index, total):
+            at = rows_at(index)
+            value = 0.9 * mom[at, :] + 0.1 * grad[at, :].astype(jnp.float32)
+            mom[at, :] = value
+            return total + jnp.abs(value)
+
+        total = lax.fori_loop(0, WORKERS, moment, jnp.zeros((rows, width), jnp.float32))
+        scale = jnp.sum(total, axis=(0, 1), keepdims=True) / (rows * WORKERS * width) + 1e-06
+        unscale = 1.0 / scale
+
+        def compress(index, carry):
+            at = rows_at(index)
+            value = mom[at, :]
+            code = (scale * jnp.tanh(value * unscale)).astype(jnp.bfloat16)
+            if sent is not None:
+                sent[at, :] = code
+            werrbuf[at, :] = value - code.astype(jnp.float32)
+            return carry
+
+        lax.fori_loop(0, WORKERS, compress, 0)
+
     kvbuf[0] = (dkt[...] * inv_root).astype(jnp.bfloat16).T
     kvbuf[1] = dvt[...].astype(jnp.bfloat16).T
 
@@ -587,8 +630,14 @@
 
     for key in q_keys:
         unless(q_mine(*key), q_copy(*key, 0).wait_send)
-    for copy in gather.every() + starts + m_copies:
+    for copy in gather.every() + m_copies:
         copy.wait_send()
+
+    @pl.when(home)
+    def _():
+        for copy in starts:
+            copy.wait_send()
+
     for slot in range(7):
         sync_copy(slot, worker, other).wait_send()
 

time: 112 us -> 112 us (level)
  no operation moved by 1% of the time
where the time goes in v7:
time: 112 us
  Pallas kernels  111 us (99%)
    pallas_call x1, Pallas kernels, body(): pl.pallas_call(functools.partial(kernel, inv_root), out_shape=(jax.ShapeD...  108 us
    pallas_call x1, Pallas kernels, body(): pl.pallas_call(finish, out_shape=(jax.ShapeDtypeStruct((3, tokens, HEADS,...  3.45 us

profile of v7, /device:TPU:1, one launch (start us, length us, event | category | flops | bytes accessed | tf_op | source)
XLA Modules:
  0.0 111.8 jit_solution(11203244643607854078)
XLA Ops:
  0.6 107.7 %shard_map.84 = (bf16[3,128,16,128]{3,2,1,0:T(8,128)(2,1)}, bf16[128,3072]{1,0:T(8,128)(2,1)}, f32[128,3072]{1,0:T(8,128)}, f32[16,3072]{1,0:T(8,128)}) custom-call(bf16[3,128,16,128]{3,2,1,0:T(8,128)(2,1)} %bitcast.10, bf16[128,3072]{1,0:T(8,128)(2,1)} %bitcast.12, bf16[128,3072]{1,0:T(8,128)(2,1)} %bitcast.13, s32[8,16,16]{2,1,0:T(8,128)} %mask_ref.1, ...), custom_call_target="tpu_custom_call" | custom-call | tf_op jit(solution)/shard_map/pallas_call | solution.py:700
  108.4 3.5 %shard_map.85 = (bf16[3,128,16,128]{3,2,1,0:T(8,128)(2,1)}, bf16[128,3072]{1,0:T(8,128)(2,1)}, f32[128,3072]{1,0:T(8,128)}, f32[16,3072]{1,0:T(8,128)}) custom-call(bf16[3,128,16,128]{3,2,1,0:T(8,128)(2,1)} %get-tuple-element.12.grads_in, bf16[128,3072]{1,0:T(8,128)(2,1)} %get-tuple-element.13.sync_in, f32[128,3072]{1,0:T(8,128)} %get-tuple-element.14.werr_in, ...), custom_call_target="tpu_custom_call" | custom-call | tf_op jit(solution)/shard_map/pallas_call | solution.py:750
